TPU v7x, 256 devices: a whole 4x4x8 slice. The times are simulated.
256 devices in a mesh: shot: 8 (over x_hi, y), box: 32 (over x_lo, z, core).
Axes of the slice: x: 4 (x_hi: 2, x_lo: 2; x = x_hi * 2 + x_lo), y: 4, z: 8, core: 2. Of those that a mesh axis runs over, the one named last changes fastest.
Arguments:
- u_prev: float32 [8, 8, 2048, 256], P('shot', None, 'box'), may hold values from -6 to 6
- u_now: float32 [8, 8, 2048, 256], P('shot', None, 'box'), may hold values from -6 to 6
- born_prev: float32 [8, 8, 2048, 256], P('shot', None, 'box'), may hold values from -6 to 6
- born_now: float32 [8, 8, 2048, 256], P('shot', None, 'box'), may hold values from -6 to 6
- adj_after: float32 [8, 8, 2048, 256], P('shot', None, 'box'), may hold values from -6 to 6
- adj_last: float32 [8, 8, 2048, 256], P('shot', None, 'box'), may hold values from -6 to 6
- velocity: float32 [8, 2048, 256], P('shot', 'box'), may hold values from 0.08 to 0.45
- wavelet: float32 [8, 8, 4], P('shot'), may hold values from -12 to 12
- sources: int32 [8, 8], P('shot'), may hold values from 0 to 524287
- receivers: int32 [8, 1024], P('shot', 'box'), may hold values from 0 to 524095, as said below
- observed: float32 [8, 8, 4, 1024], P('shot', None, None, 'box'), may hold values from -6 to 6
- first_tile: int32 [8], P('shot'), may hold values from 0 to 256
- reflectivity: float32 [40, 32, 2, 256], P(None, 'box'), may hold values from -6 to 6
Outputs:
- migrated: float32 [40, 32, 2, 256], P(None, 'box')
Inputs may be any that keep to these rules, and one draw needn't show every extreme that they name: `receivers`: receiver r of every group lies in the grid columns r * 2 to (r + 1) * 2 - 1 of its box, at a depth cell under 256 // 4.
All inputs are finite; a program needn't handle non-finite values.
Results may differ from a plain program's by a relative error of at most 0.00011.
Values sent between devices are 32-bit elements; how exact they have to be, the bound alone decides.
A program may use at most 64 MiB of HBM per device.

v0:
```python
import jax
import jax.numpy as jnp
from jax import lax
from jax.sharding import PartitionSpec as P

damping = 1.0


def padded_2(block, sides, width):
    for axis, dim in sides:
        count = lax.axis_size(axis)
        forward = [(i, i + 1) for i in range(count - 1)]
        backward = [(target, source) for source, target in forward]
        low = lax.ppermute(
            lax.slice_in_dim(block, block.shape[dim] - width, None, axis=dim), axis, forward
        )
        high = lax.ppermute(lax.slice_in_dim(block, 0, width, axis=dim), axis, backward)
        block = jnp.concatenate([low, block, high], axis=dim)
    return block


def laplace_rows(padded):
    center = padded[:, 1:-1]
    deeper = jnp.pad(center, ((0, 0), (0, 0), (1, 1)))
    return padded[:, 2:] + padded[:, :-2] + deeper[:, :, 2:] + deeper[:, :, :-2] - 4.0 * center


def on_device(
    u_prev,
    u_now,
    born_prev,
    born_now,
    adj_after,
    adj_last,
    velocity,
    wavelet,
    sources,
    receivers,
    observed,
    first_tile,
    reflectivity,
):
    owners = lax.axis_size("box")
    position = lax.axis_index("box")
    shot_count = u_now.shape[1]
    columns = u_now.shape[2]
    depth_cells = u_now.shape[3]
    step_count = wavelet.shape[2]
    tile_width = reflectivity.shape[2]
    start_tile = first_tile[0]
    round_base = start_tile // owners
    rotation = start_tile % owners
    first_round = round_base + (position < rotation).astype(jnp.int32)
    owned_tiles = reflectivity[:, 0]
    outgoing = lax.dynamic_slice_in_dim(owned_tiles, first_round, owners, 0)
    incoming = lax.all_to_all(outgoing, "box", split_axis=0, concat_axis=0, tiled=True)
    image_slab = jnp.roll(incoming, -rotation, axis=0).reshape(columns, depth_cells)
    speed_slab = velocity[0]
    column_start = position * columns
    source_column = sources[0] // depth_cells - column_start
    source_depth = sources[0] % depth_cells
    receiver_global = receivers[0] // depth_cells
    receiver_column = receiver_global - column_start
    receiver_depth = receivers[0] % depth_cells
    pulses = wavelet[0]
    recorded = observed[0]
    shot_lane = jnp.arange(shot_count, dtype=jnp.int32)
    accelerations = []
    predicted = []
    gradient = jnp.zeros((columns, depth_cells), jnp.float32)
    illumination = jnp.zeros((columns, depth_cells), jnp.float32)
    older_u, newer_u = (u_prev[0], u_now[0])
    older_b, newer_b = (born_prev[0], born_now[0])
    for moment in range(step_count):
        joined = jnp.concatenate([newer_u, newer_b], axis=0)
        padded = padded_2(joined, (("box", 1),), 1)
        lap_all = laplace_rows(padded)
        next_u = 2.0 * newer_u - older_u + speed_slab * lap_all[:shot_count]
        column = source_column
        inside = (column >= 0) & (column < next_u.shape[1])
        column = jnp.clip(column, 0, next_u.shape[1] - 1)
        next_u = next_u.at[shot_lane, column, source_depth].add(
            jnp.where(inside, pulses[:, moment], 0.0)
        )
        second_diff = next_u - 2.0 * newer_u + older_u
        next_b = (
            2.0 * newer_b - older_b + speed_slab * lap_all[shot_count:] + image_slab * second_diff
        )
        accelerations.append(second_diff)
        predicted.append(next_b[:, receiver_column, receiver_depth])
        older_u, newer_u = (newer_u, next_u)
        older_b, newer_b = (newer_b, next_b)
    adjoint_old, adjoint_new = (adj_after[0], adj_last[0])
    for moment in reversed(range(step_count)):
        padded_adjoint = padded_2(adjoint_new, (("box", 1),), 1)
        adjoint_next = 2.0 * adjoint_new - adjoint_old + speed_slab * laplace_rows(padded_adjoint)
        misfit = predicted[moment] - recorded[:, moment, :]
        adjoint_next = adjoint_next.at[:, receiver_column, receiver_depth].add(misfit)
        gradient = gradient + jnp.sum(adjoint_next * accelerations[moment], axis=0)
        illumination = illumination + jnp.sum(accelerations[moment] * accelerations[moment], axis=0)
        adjoint_old, adjoint_new = (adjoint_new, adjoint_next)

    def to_owner(slab_values):
        blocks = slab_values.reshape(owners, tile_width, depth_cells)
        return jnp.roll(blocks, rotation, axis=0)

    back_grad, back_illum = (
        lax.all_to_all(to_owner(gradient), "box", split_axis=0, concat_axis=0, tiled=True),
        lax.all_to_all(to_owner(illumination), "box", split_axis=0, concat_axis=0, tiled=True),
    )
    empty_rounds = jnp.zeros(owned_tiles.shape, jnp.float32)
    grad_rounds = lax.dynamic_update_slice_in_dim(empty_rounds, back_grad, first_round, 0)
    illum_rounds = lax.dynamic_update_slice_in_dim(empty_rounds, back_illum, first_round, 0)
    total_grad, total_illum = lax.psum((grad_rounds, illum_rounds), "shot")
    migrated = total_grad / jnp.sqrt(total_illum + damping)
    return migrated[:, None]


def solution(mesh):
    return jax.shard_map(
        on_device,
        mesh=mesh,
        in_specs=(
            P("shot", None, "box", None),
            P("shot", None, "box", None),
            P("shot", None, "box", None),
            P("shot", None, "box", None),
            P("shot", None, "box", None),
            P("shot", None, "box", None),
            P("shot", "box", None),
            P("shot", None, None),
            P("shot", None),
            P("shot", "box"),
            P("shot", None, None, "box"),
            P("shot"),
            P(None, "box", None, None),
        ),
        out_specs=P(None, "box", None, None),
        check_vma=False,
    )
```

profile of v0, /device:TPU:1, one launch (start us, length us, event | category | flops | bytes accessed | tf_op | source)
XLA Modules:
  0.0 320.4 jit_solution(5495484784613867335)
XLA Ops:
  8.1 11.0 %all-to-all-start = ((f32[32,2,256]{2,1,0:T(2,128)}), f32[32,2,256]{2,1,0:T(2,128)S(1)}, u32[]{:S(2)}, u32[]{:S(2)}) async-start(f32[32,2,256]{2,1,0:T(2,128)} %dynamic-slice_bitcast_fusion), calls=%async_computation | async-start | bytes 131072 | tf_op jit(solution)/shard_map/all_to_all | solution.py:56
  20.1 2.1 collective-permute-start.2
  22.2 3.4 %collective-permute-start.3 = (f32[16,1,256]{2,1,0:T(1,128)S(1)}, f32[16,1,256]{2,1,0:T(1,128)S(1)}, u32[]{:S(2)}, u32[]{:S(2)}) collective-permute-start(f32[16,1,256]{2,1,0:T(1,128)S(1)} %get-tuple-element.36), channel_id=1, source_target_pairs={{0,1},{1,2},{2,3},{3,4},{4,5},{5,6},{6,7},{7,8},{8,9},{9,10},{10,1... | collective-permute-start | bytes 49160 | tf_op jit(solution)/shard_map/ppermute | solution.py:14
  26.5 1.9 collective-permute-start
  28.5 3.6 %collective-permute-start.1 = (f32[8,1,256]{2,1,0:T(1,128)S(1)}, f32[8,1,256]{2,1,0:T(1,128)S(1)}, u32[]{:S(2)}, u32[]{:S(2)}) collective-permute-start(f32[8,1,256]{2,1,0:T(1,128)S(1)} %get-tuple-element.48), channel_id=1, source_target_pairs={{0,1},{1,2},{2,3},{3,4},{4,5},{5,6},{6,7},{7,8},{8,9},{9,10},{10,1... | collective-permute-start | bytes 24584 | tf_op jit(solution)/shard_map/ppermute | solution.py:14
  37.1 2.3 fusion.2
  39.4 1.7 fusion.48
  42.3 2.4 fusion.50
  44.7 1.9 collective-permute-start.4
  46.6 3.6 %collective-permute-start.5 = (f32[16,1,256]{2,1,0:T(1,128)S(1)}, f32[16,1,256]{2,1,0:T(1,128)S(1)}, u32[]{:S(2)}, u32[]{:S(2)}) collective-permute-start(f32[16,1,256]{2,1,0:T(1,128)S(1)} %get-tuple-element.34), channel_id=1, source_target_pairs={{0,1},{1,2},{2,3},{3,4},{4,5},{5,6},{6,7},{7,8},{8,9},{9,10},{10,1... | collective-permute-start | bytes 49160 | tf_op jit(solution)/shard_map/ppermute | solution.py:14
  51.5 4.6 %copy.47 = f32[8,64,256]{0,2,1:T(8,128)} copy(f32[8,64,256]{2,1,0:T(8,128)S(1)} %get-tuple-element.27) | data formatting | bytes 1048576 | tf_op jit(solution)/shard_map/add | solution.py:87
  57.4 2.8 fusion.5
  62.2 2.1 fusion.47
  64.3 1.9 collective-permute-start.6
  66.2 3.6 %collective-permute-start.7 = (f32[16,1,256]{2,1,0:T(1,128)S(1)}, f32[16,1,256]{2,1,0:T(1,128)S(1)}, u32[]{:S(2)}, u32[]{:S(2)}) collective-permute-start(f32[16,1,256]{2,1,0:T(1,128)S(1)} %get-tuple-element.32), channel_id=1, source_target_pairs={{0,1},{1,2},{2,3},{3,4},{4,5},{5,6},{6,7},{7,8},{8,9},{9,10},{10,1... | collective-permute-start | bytes 49160 | tf_op jit(solution)/shard_map/ppermute | solution.py:14
  71.0 4.6 %copy.36 = f32[8,64,256]{0,2,1:T(8,128)} copy(f32[8,64,256]{2,1,0:T(8,128)S(1)} %get-tuple-element.25) | data formatting | bytes 1048576 | tf_op jit(solution)/shard_map/add | solution.py:87
  76.9 2.8 fusion.8
  81.7 2.1 fusion.44
  83.8 1.9 collective-permute-start.8
  85.7 3.8 %collective-permute-start.9 = (f32[16,1,256]{2,1,0:T(1,128)S(1)}, f32[16,1,256]{2,1,0:T(1,128)S(1)}, u32[]{:S(2)}, u32[]{:S(2)}) collective-permute-start(f32[16,1,256]{2,1,0:T(1,128)S(1)} %get-tuple-element.30), channel_id=1, source_target_pairs={{0,1},{1,2},{2,3},{3,4},{4,5},{5,6},{6,7},{7,8},{8,9},{9,10},{10,1... | collective-permute-start | bytes 49160 | tf_op jit(solution)/shard_map/ppermute | solution.py:14
  90.7 4.6 %copy.25 = f32[8,64,256]{0,2,1:T(8,128)} copy(f32[8,64,256]{2,1,0:T(8,128)S(1)} %get-tuple-element.23) | data formatting | bytes 1048576 | tf_op jit(solution)/shard_map/add | solution.py:87
  96.6 2.8 fusion.11
  101.4 3.0 fusion.41
  104.5 5.9 %copy.14 = f32[8,64,256]{0,2,1:T(8,128)} copy(f32[8,64,256]{2,1,0:T(8,128)} %get-tuple-element.19) | data formatting | bytes 1048576 | tf_op jit(solution)/shard_map/add | solution.py:87
  111.7 4.6 %copy.16 = f32[8,64,256]{0,2,1:T(8,128)} copy(f32[8,64,256]{2,1,0:T(8,128)S(1)} %copy-done.10) | data formatting | bytes 1048576 | tf_op jit(solution)/shard_map/add | solution.py:96
  116.3 3.7 %scatter_fusion.4 = f32[8,64,256]{0,2,1:T(8,128)} fusion(f32[8,64,256]{0,2,1:T(8,128)} %copy.16, s32[32]{0:T(128)S(1)} %fusion.76, f32[32,8]{1,0:T(8,128)S(1)} %get-tuple-element.52), kind=kCustom, calls=%fused_computation.8 | custom fusion | flops 256 | bytes 3328 | tf_op jit(solution)/shard_map/scatter-add | solution.py:98
  120.1 5.2 %copy.17 = f32[8,64,256]{2,1,0:T(8,128)S(1)} copy(f32[8,64,256]{0,2,1:T(8,128)} %scatter_fusion.4) | data formatting | bytes 1048576 | tf_op jit(solution)/shard_map/scatter-add | solution.py:98
  125.2 1.9 collective-permute-start.10
  127.2 3.8 %collective-permute-start.11 = (f32[8,1,256]{2,1,0:T(1,128)S(1)}, f32[8,1,256]{2,1,0:T(1,128)S(1)}, u32[]{:S(2)}, u32[]{:S(2)}) collective-permute-start(f32[8,1,256]{2,1,0:T(1,128)S(1)} %get-tuple-element.46), channel_id=1, source_target_pairs={{0,1},{1,2},{2,3},{3,4},{4,5},{5,6},{6,7},{7,8},{8,9},{9,10},{10,1... | collective-permute-start | bytes 24584 | tf_op jit(solution)/shard_map/ppermute | solution.py:14
  132.0 4.6 %copy.26 = f32[8,64,256]{0,2,1:T(8,128)} copy(f32[8,64,256]{2,1,0:T(8,128)S(1)} %fusion.25) | data formatting | bytes 1048576 | tf_op jit(solution)/shard_map/add | solution.py:96
  136.6 3.7 %scatter_fusion.5 = f32[8,64,256]{0,2,1:T(8,128)} fusion(f32[8,64,256]{0,2,1:T(8,128)} %copy.26, s32[32]{0:T(128)S(1)} %fusion.76, f32[32,8]{1,0:T(8,128)S(1)} %get-tuple-element.51), kind=kCustom, calls=%fused_computation.9 | custom fusion | flops 256 | bytes 3328 | tf_op jit(solution)/shard_map/scatter-add | solution.py:98
  140.3 5.2 %copy.27 = f32[8,64,256]{2,1,0:T(8,128)S(1)} copy(f32[8,64,256]{0,2,1:T(8,128)} %scatter_fusion.5) | data formatting | bytes 1048576 | tf_op jit(solution)/shard_map/scatter-add | solution.py:98
  145.5 1.9 collective-permute-start.12
  147.4 4.2 %collective-permute-start.13 = (f32[8,1,256]{2,1,0:T(1,128)S(1)}, f32[8,1,256]{2,1,0:T(1,128)S(1)}, u32[]{:S(2)}, u32[]{:S(2)}) collective-permute-start(f32[8,1,256]{2,1,0:T(1,128)S(1)} %get-tuple-element.44), channel_id=1, source_target_pairs={{0,1},{1,2},{2,3},{3,4},{4,5},{5,6},{6,7},{7,8},{8,9},{9,10},{10,1... | collective-permute-start | bytes 24584 | tf_op jit(solution)/shard_map/ppermute | solution.py:14
  152.9 4.6 %copy.37 = f32[8,64,256]{0,2,1:T(8,128)} copy(f32[8,64,256]{2,1,0:T(8,128)S(1)} %get-tuple-element.40) | data formatting | bytes 1048576 | tf_op jit(solution)/shard_map/add | solution.py:96
  157.5 3.7 %scatter_fusion.6 = f32[8,64,256]{0,2,1:T(8,128)} fusion(f32[8,64,256]{0,2,1:T(8,128)} %copy.37, s32[32]{0:T(128)S(1)} %fusion.76, f32[32,8]{1,0:T(8,128)S(1)} %get-tuple-element.50), kind=kCustom, calls=%fused_computation.10 | custom fusion | flops 256 | bytes 3328 | tf_op jit(solution)/shard_map/scatter-add | solution.py:98
  161.2 5.2 %copy.38 = f32[8,64,256]{2,1,0:T(8,128)S(1)} copy(f32[8,64,256]{0,2,1:T(8,128)} %scatter_fusion.6) | data formatting | bytes 1048576 | tf_op jit(solution)/shard_map/scatter-add | solution.py:98
  166.4 1.9 collective-permute-start.14
  168.3 4.2 %collective-permute-start.15 = (f32[8,1,256]{2,1,0:T(1,128)S(1)}, f32[8,1,256]{2,1,0:T(1,128)S(1)}, u32[]{:S(2)}, u32[]{:S(2)}) collective-permute-start(f32[8,1,256]{2,1,0:T(1,128)S(1)} %get-tuple-element.42), channel_id=1, source_target_pairs={{0,1},{1,2},{2,3},{3,4},{4,5},{5,6},{6,7},{7,8},{8,9},{9,10},{10,1... | collective-permute-start | bytes 24584 | tf_op jit(solution)/shard_map/ppermute | solution.py:14
  173.8 4.6 %copy.48 = f32[8,64,256]{0,2,1:T(8,128)} copy(f32[8,64,256]{2,1,0:T(8,128)S(1)} %get-tuple-element.37) | data formatting | bytes 1048576 | tf_op jit(solution)/shard_map/add | solution.py:96
  178.4 3.7 %scatter_fusion.7 = f32[8,64,256]{0,2,1:T(8,128)} fusion(f32[8,64,256]{0,2,1:T(8,128)} %copy.48, s32[32]{0:T(128)S(1)} %fusion.76, f32[32,8]{1,0:T(8,128)S(1)} %get-tuple-element.49), kind=kCustom, calls=%fused_computation.11 | custom fusion | flops 256 | bytes 3328 | tf_op jit(solution)/shard_map/scatter-add | solution.py:98
  182.1 5.2 %copy.49 = f32[8,64,256]{2,1,0:T(8,128)S(1)} copy(f32[8,64,256]{0,2,1:T(8,128)} %scatter_fusion.7) | data formatting | bytes 1048576 | tf_op jit(solution)/shard_map/scatter-add | solution.py:98
  188.2 23.4 %all-to-all-start.2 = ((f32[32,2,256]{2,1,0:T(2,128)}), f32[32,2,256]{2,1,0:T(2,128)S(1)}, u32[]{:S(2)}, u32[]{:S(2)}) async-start(f32[32,2,256]{2,1,0:T(2,128)} %fusion.52), calls=%async_computation.2 | async-start | bytes 131072 | tf_op jit(solution)/shard_map/all_to_all | solution.py:109
  212.4 7.2 %all-to-all-done.2 = f32[32,2,256]{2,1,0:T(2,128)S(1)} async-done(((f32[32,2,256]{2,1,0:T(2,128)}), f32[32,2,256]{2,1,0:T(2,128)S(1)}, u32[]{:S(2)}, u32[]{:S(2)}) %all-to-all-start.2) | async-done | bytes 65568 | tf_op jit(solution)/shard_map/all_to_all | solution.py:109
  219.6 4.8 %all-to-all-start.1 = ((f32[32,2,256]{2,1,0:T(2,128)}), f32[32,2,256]{2,1,0:T(2,128)S(1)}, u32[]{:S(2)}, u32[]{:S(2)}) async-start(f32[32,2,256]{2,1,0:T(2,128)} %fusion.53), calls=%async_computation.1 | async-start | bytes 131072 | tf_op jit(solution)/shard_map/all_to_all | solution.py:108
  224.5 8.1 %all-to-all-done.1 = f32[32,2,256]{2,1,0:T(2,128)S(1)} async-done(((f32[32,2,256]{2,1,0:T(2,128)}), f32[32,2,256]{2,1,0:T(2,128)S(1)}, u32[]{:S(2)}, u32[]{:S(2)}) %all-to-all-start.1) | async-done | bytes 65568 | tf_op jit(solution)/shard_map/all_to_all | solution.py:108
  233.3 78.6 %all-reduce.11.cloned.1.call-done = (f32[40,2,256]{2,1,0:T(2,128)}, f32[40,2,256]{2,1,0:T(2,128)}) async-done(((f32[40,2,256]{2,1,0:T(2,128)}, f32[40,2,256]{2,1,0:T(2,128)}), (f32[40,2,256]{2,1,0:T(2,128)}, f32[40,2,256]{2,1,0:T(2,128)})) %all-reduce.11.cloned.1.call-update) | async-done | bytes 163856 | tf_op jit(solution)/shard_map/psum | solution.py:114
  311.9 1.6 multiply_bitcast_fusion
  (99 shorter events, 29.1 us)
Async XLA Ops:
  6.5 0.9 copy-start
  6.5 35.7 %copy-start.3 = (f32[1,8,64,256]{3,2,1,0:T(8,128)S(1)}, f32[1,8,64,256]{3,2,1,0:T(8,128)}, u32[]{:S(2)}) copy-start(f32[1,8,64,256]{3,2,1,0:T(8,128)} %param.18) | copy-start | bytes 1572868
  6.5 35.7 %copy-start.2 = (f32[1,8,64,256]{3,2,1,0:T(8,128)S(1)}, f32[1,8,64,256]{3,2,1,0:T(8,128)}, u32[]{:S(2)}) copy-start(f32[1,8,64,256]{3,2,1,0:T(8,128)} %param.16) | copy-start | bytes 1572868
  6.5 35.7 %copy-start.4 = (f32[1,64,256]{2,1,0:T(8,128)S(1)}, f32[1,64,256]{2,1,0:T(8,128)}, u32[]{:S(2)}) copy-start(f32[1,64,256]{2,1,0:T(8,128)} %param.21) | copy-start | bytes 196612
  8.1 34.0 %all-to-all-start = ((f32[32,2,256]{2,1,0:T(2,128)}), f32[32,2,256]{2,1,0:T(2,128)S(1)}, u32[]{:S(2)}, u32[]{:S(2)}) async-start(f32[32,2,256]{2,1,0:T(2,128)} %dynamic-slice_bitcast_fusion), calls=%async_computation | async-start | bytes 131072 | tf_op jit(solution)/shard_map/all_to_all | solution.py:56
  20.1 17.0 %collective-permute-start.2 = (f32[16,1,256]{2,1,0:T(1,128)S(1)}, f32[16,1,256]{2,1,0:T(1,128)S(1)}, u32[]{:S(2)}, u32[]{:S(2)}) collective-permute-start(f32[16,1,256]{2,1,0:T(1,128)S(1)} %get-tuple-element.35), channel_id=1, source_target_pairs={{1,0},{2,1},{3,2},{4,3},{5,4},{6,5},{7,6},{8,7},{9,8},{10,9},{11,1... | collective-permute-start | bytes 49160 | tf_op jit(solution)/shard_map/ppermute | solution.py:17
  22.2 14.9 %collective-permute-start.3 = (f32[16,1,256]{2,1,0:T(1,128)S(1)}, f32[16,1,256]{2,1,0:T(1,128)S(1)}, u32[]{:S(2)}, u32[]{:S(2)}) collective-permute-start(f32[16,1,256]{2,1,0:T(1,128)S(1)} %get-tuple-element.36), channel_id=1, source_target_pairs={{0,1},{1,2},{2,3},{3,4},{4,5},{5,6},{6,7},{7,8},{8,9},{9,10},{10,1... | collective-permute-start | bytes 49160 | tf_op jit(solution)/shard_map/ppermute | solution.py:14
  26.5 74.9 %collective-permute-start = (f32[8,1,256]{2,1,0:T(1,128)S(1)}, f32[8,1,256]{2,1,0:T(1,128)S(1)}, u32[]{:S(2)}, u32[]{:S(2)}) collective-permute-start(f32[8,1,256]{2,1,0:T(1,128)S(1)} %get-tuple-element.47), channel_id=1, source_target_pairs={{1,0},{2,1},{3,2},{4,3},{5,4},{6,5},{7,6},{8,7},{9,8},{10,9},{11,1... | collective-permute-start | bytes 24584 | tf_op jit(solution)/shard_map/ppermute | solution.py:17
  28.5 72.9 %collective-permute-start.1 = (f32[8,1,256]{2,1,0:T(1,128)S(1)}, f32[8,1,256]{2,1,0:T(1,128)S(1)}, u32[]{:S(2)}, u32[]{:S(2)}) collective-permute-start(f32[8,1,256]{2,1,0:T(1,128)S(1)} %get-tuple-element.48), channel_id=1, source_target_pairs={{0,1},{1,2},{2,3},{3,4},{4,5},{5,6},{6,7},{7,8},{8,9},{9,10},{10,1... | collective-permute-start | bytes 24584 | tf_op jit(solution)/shard_map/ppermute | solution.py:14
  39.4 2.8 copy-start.6
  44.7 12.7 %collective-permute-start.4 = (f32[16,1,256]{2,1,0:T(1,128)S(1)}, f32[16,1,256]{2,1,0:T(1,128)S(1)}, u32[]{:S(2)}, u32[]{:S(2)}) collective-permute-start(f32[16,1,256]{2,1,0:T(1,128)S(1)} %get-tuple-element.33), channel_id=1, source_target_pairs={{1,0},{2,1},{3,2},{4,3},{5,4},{6,5},{7,6},{8,7},{9,8},{10,9},{11,1... | collective-permute-start | bytes 49160 | tf_op jit(solution)/shard_map/ppermute | solution.py:17
  46.6 10.8 %collective-permute-start.5 = (f32[16,1,256]{2,1,0:T(1,128)S(1)}, f32[16,1,256]{2,1,0:T(1,128)S(1)}, u32[]{:S(2)}, u32[]{:S(2)}) collective-permute-start(f32[16,1,256]{2,1,0:T(1,128)S(1)} %get-tuple-element.34), channel_id=1, source_target_pairs={{0,1},{1,2},{2,3},{3,4},{4,5},{5,6},{6,7},{7,8},{8,9},{9,10},{10,1... | collective-permute-start | bytes 49160 | tf_op jit(solution)/shard_map/ppermute | solution.py:14
  60.3 1.0 copy-start.8
  64.3 12.7 %collective-permute-start.6 = (f32[16,1,256]{2,1,0:T(1,128)S(1)}, f32[16,1,256]{2,1,0:T(1,128)S(1)}, u32[]{:S(2)}, u32[]{:S(2)}) collective-permute-start(f32[16,1,256]{2,1,0:T(1,128)S(1)} %get-tuple-element.31), channel_id=1, source_target_pairs={{1,0},{2,1},{3,2},{4,3},{5,4},{6,5},{7,6},{8,7},{9,8},{10,9},{11,1... | collective-permute-start | bytes 49160 | tf_op jit(solution)/shard_map/ppermute | solution.py:17
  66.2 10.8 %collective-permute-start.7 = (f32[16,1,256]{2,1,0:T(1,128)S(1)}, f32[16,1,256]{2,1,0:T(1,128)S(1)}, u32[]{:S(2)}, u32[]{:S(2)}) collective-permute-start(f32[16,1,256]{2,1,0:T(1,128)S(1)} %get-tuple-element.32), channel_id=1, source_target_pairs={{0,1},{1,2},{2,3},{3,4},{4,5},{5,6},{6,7},{7,8},{8,9},{9,10},{10,1... | collective-permute-start | bytes 49160 | tf_op jit(solution)/shard_map/ppermute | solution.py:14
  79.8 1.0 copy-start.7
  83.8 12.8 %collective-permute-start.8 = (f32[16,1,256]{2,1,0:T(1,128)S(1)}, f32[16,1,256]{2,1,0:T(1,128)S(1)}, u32[]{:S(2)}, u32[]{:S(2)}) collective-permute-start(f32[16,1,256]{2,1,0:T(1,128)S(1)} %get-tuple-element.29), channel_id=1, source_target_pairs={{1,0},{2,1},{3,2},{4,3},{5,4},{6,5},{7,6},{8,7},{9,8},{10,9},{11,1... | collective-permute-start | bytes 49160 | tf_op jit(solution)/shard_map/ppermute | solution.py:17
  85.7 15.7 %copy-start.9 = (f32[1,8,64,256]{3,2,1,0:T(8,128)S(1)}, f32[1,8,64,256]{3,2,1,0:T(8,128)}, u32[]{:S(2)}) copy-start(f32[1,8,64,256]{3,2,1,0:T(8,128)} %param.20) | copy-start | bytes 1572868
  85.7 10.9 %collective-permute-start.9 = (f32[16,1,256]{2,1,0:T(1,128)S(1)}, f32[16,1,256]{2,1,0:T(1,128)S(1)}, u32[]{:S(2)}, u32[]{:S(2)}) collective-permute-start(f32[16,1,256]{2,1,0:T(1,128)S(1)} %get-tuple-element.30), channel_id=1, source_target_pairs={{0,1},{1,2},{2,3},{3,4},{4,5},{5,6},{6,7},{7,8},{8,9},{9,10},{10,1... | collective-permute-start | bytes 49160 | tf_op jit(solution)/shard_map/ppermute | solution.py:14
  99.5 1.0 copy-start.5
  104.5 7.3 %copy-start.10 = (f32[8,64,256]{2,1,0:T(8,128)S(1)}, f32[8,64,256]{2,1,0:T(8,128)}, u32[]{:S(2)}) copy-start(f32[8,64,256]{2,1,0:T(8,128)} %get-tuple-element.53) | copy-start | bytes 1572868
  125.2 5.8 %collective-permute-start.10 = (f32[8,1,256]{2,1,0:T(1,128)S(1)}, f32[8,1,256]{2,1,0:T(1,128)S(1)}, u32[]{:S(2)}, u32[]{:S(2)}) collective-permute-start(f32[8,1,256]{2,1,0:T(1,128)S(1)} %get-tuple-element.45), channel_id=1, source_target_pairs={{1,0},{2,1},{3,2},{4,3},{5,4},{6,5},{7,6},{8,7},{9,8},{10,9},{11,1... | collective-permute-start | bytes 24584 | tf_op jit(solution)/shard_map/ppermute | solution.py:17
  127.2 4.4 %collective-permute-start.11 = (f32[8,1,256]{2,1,0:T(1,128)S(1)}, f32[8,1,256]{2,1,0:T(1,128)S(1)}, u32[]{:S(2)}, u32[]{:S(2)}) collective-permute-start(f32[8,1,256]{2,1,0:T(1,128)S(1)} %get-tuple-element.46), channel_id=1, source_target_pairs={{0,1},{1,2},{2,3},{3,4},{4,5},{5,6},{6,7},{7,8},{8,9},{9,10},{10,1... | collective-permute-start | bytes 24584 | tf_op jit(solution)/shard_map/ppermute | solution.py:14
  132.0 20.4 %copy-start.14 = (f32[8,64,256]{2,1,0:T(8,128)S(1)}, f32[8,64,256]{2,1,0:T(8,128)}, u32[]{:S(2)}) copy-start(f32[8,64,256]{2,1,0:T(8,128)} %get-tuple-element.20) | copy-start | bytes 1572868
  145.5 6.2 %collective-permute-start.12 = (f32[8,1,256]{2,1,0:T(1,128)S(1)}, f32[8,1,256]{2,1,0:T(1,128)S(1)}, u32[]{:S(2)}, u32[]{:S(2)}) collective-permute-start(f32[8,1,256]{2,1,0:T(1,128)S(1)} %get-tuple-element.43), channel_id=1, source_target_pairs={{1,0},{2,1},{3,2},{4,3},{5,4},{6,5},{7,6},{8,7},{9,8},{10,9},{11,1... | collective-permute-start | bytes 24584 | tf_op jit(solution)/shard_map/ppermute | solution.py:17
  147.4 5.0 %collective-permute-start.13 = (f32[8,1,256]{2,1,0:T(1,128)S(1)}, f32[8,1,256]{2,1,0:T(1,128)S(1)}, u32[]{:S(2)}, u32[]{:S(2)}) collective-permute-start(f32[8,1,256]{2,1,0:T(1,128)S(1)} %get-tuple-element.44), channel_id=1, source_target_pairs={{0,1},{1,2},{2,3},{3,4},{4,5},{5,6},{6,7},{7,8},{8,9},{9,10},{10,1... | collective-permute-start | bytes 24584 | tf_op jit(solution)/shard_map/ppermute | solution.py:14
  152.9 20.5 %copy-start.12 = (f32[8,64,256]{2,1,0:T(8,128)S(1)}, f32[8,64,256]{2,1,0:T(8,128)}, u32[]{:S(2)}) copy-start(f32[8,64,256]{2,1,0:T(8,128)} %get-tuple-element.26) | copy-start | bytes 1572868
  152.9 20.4 %copy-start.13 = (f32[8,64,256]{2,1,0:T(8,128)S(1)}, f32[8,64,256]{2,1,0:T(8,128)}, u32[]{:S(2)}) copy-start(f32[8,64,256]{2,1,0:T(8,128)} %get-tuple-element.24) | copy-start | bytes 1572868
  166.4 6.2 %collective-permute-start.14 = (f32[8,1,256]{2,1,0:T(1,128)S(1)}, f32[8,1,256]{2,1,0:T(1,128)S(1)}, u32[]{:S(2)}, u32[]{:S(2)}) collective-permute-start(f32[8,1,256]{2,1,0:T(1,128)S(1)} %get-tuple-element.41), channel_id=1, source_target_pairs={{1,0},{2,1},{3,2},{4,3},{5,4},{6,5},{7,6},{8,7},{9,8},{10,9},{11,1... | collective-permute-start | bytes 24584 | tf_op jit(solution)/shard_map/ppermute | solution.py:17
  168.3 5.0 %collective-permute-start.15 = (f32[8,1,256]{2,1,0:T(1,128)S(1)}, f32[8,1,256]{2,1,0:T(1,128)S(1)}, u32[]{:S(2)}, u32[]{:S(2)}) collective-permute-start(f32[8,1,256]{2,1,0:T(1,128)S(1)} %get-tuple-element.42), channel_id=1, source_target_pairs={{0,1},{1,2},{2,3},{3,4},{4,5},{5,6},{6,7},{7,8},{8,9},{9,10},{10,1... | collective-permute-start | bytes 24584 | tf_op jit(solution)/shard_map/ppermute | solution.py:14
  173.8 13.5 %copy-start.11 = (f32[8,64,256]{2,1,0:T(8,128)S(1)}, f32[8,64,256]{2,1,0:T(8,128)}, u32[]{:S(2)}) copy-start(f32[8,64,256]{2,1,0:T(8,128)} %get-tuple-element.28) | copy-start | bytes 1572868
  173.8 139.8 %copy-start.1 = (f32[40,1,2,256]{3,2,1,0:T(2,128)S(1)}, f32[40,1,2,256]{3,2,1,0:T(2,128)}, u32[]{:S(2)}) copy-start(f32[40,1,2,256]{3,2,1,0:T(2,128)} %param.27) | copy-start | bytes 245764
  188.2 31.4 %all-to-all-start.2 = ((f32[32,2,256]{2,1,0:T(2,128)}), f32[32,2,256]{2,1,0:T(2,128)S(1)}, u32[]{:S(2)}, u32[]{:S(2)}) async-start(f32[32,2,256]{2,1,0:T(2,128)} %fusion.52), calls=%async_computation.2 | async-start | bytes 131072 | tf_op jit(solution)/shard_map/all_to_all | solution.py:109
  219.6 12.9 %all-to-all-start.1 = ((f32[32,2,256]{2,1,0:T(2,128)}), f32[32,2,256]{2,1,0:T(2,128)S(1)}, u32[]{:S(2)}, u32[]{:S(2)}) async-start(f32[32,2,256]{2,1,0:T(2,128)} %fusion.53), calls=%async_computation.1 | async-start | bytes 131072 | tf_op jit(solution)/shard_map/all_to_all | solution.py:108
  224.4 87.5 %all-reduce.11.cloned.1.call-start = ((), (), s32[]{:S(2)}) async-start(), calls=%async_computation.3 | async-start | bytes 327680 | tf_op jit(solution)/shard_map/psum | solution.py:114
  224.5 8.1 %copy-start.16 = (f32[40,2,256]{2,1,0:T(2,128)}, f32[40,2,256]{2,1,0:T(2,128)S(1)}, u32[]{:S(2)}) copy-start(f32[40,2,256]{2,1,0:T(2,128)S(1)} %constant_dynamic-update-slice_fusion) | copy-start | bytes 245764
  232.6 0.6 copy-start.15
Sparse Core Ops, SparseCore 0:
  233.4 78.4 all-reduce.10
where the time goes:
time: 326 us; the launch traced here: 320 us
  waiting for transfers between devices  96.1 us (29%)
  starting transfers between devices  85.2 us (26%)
  local copies, waits for them, and re-layouts  69.8 us (21%)
  other arithmetic  54.4 us (17%)
  between operations  14.9 us (5%)
    psum x1, waiting for transfers between devices, on_device(): total_grad, total_illum = lax.psum((grad_rounds, illum_rounds), 'shot')  78.6 us
    ppermute x8, starting transfers between devices, padded_2(): lax.ppermute(lax.slice_in_dim(block, block.shape[dim] - width, None, axis...  30.4 us
    all_to_all x1, starting transfers between devices, on_device(): lax.all_to_all(to_owner(illumination), 'box', split_axis=0, concat_axis=0...  23.4 us
    scatter-add x4, local copies, waits for them, and re-layouts, on_device(): adjoint_next.at[:, receiver_column, receiver_depth].add(misfit)  20.6 us
    add x4, local copies, waits for them, and re-layouts, on_device(): 2.0 * newer_b - older_b + speed_slab * lap_all[shot_count:]  19.6 us
    add x4, local copies, waits for them, and re-layouts, on_device(): 2.0 * adjoint_new - adjoint_old + speed_slab * laplace_rows(padded_adjoint)  18.3 us
    ppermute x8, starting transfers between devices, padded_2(): lax.ppermute(lax.slice_in_dim(block, 0, width, axis=dim), axis, backward)  15.6 us
    scatter-add x4, other arithmetic, on_device(): adjoint_next.at[:, receiver_column, receiver_depth].add(misfit)  14.9 us
  transfers between devices with their start and end apart: 20, of which 6 were waited for; matrix products, arithmetic and copies ran while one was open for 16% of the time, Pallas kernels for 0%

commit v1 on v0

v1 whole, which is shorter than its diff:
```python
import functools

import jax
import jax.numpy as jnp
from jax import lax
from jax.experimental import pallas as pl
from jax.experimental.pallas import tpu as pltpu
from jax.sharding import PartitionSpec as P

damping = 1.0
LANES = 128
HALO = 8
BLOCK = 8
F32 = jnp.float32
MESH = pl.DeviceIdType.MESH


def wait_bytes(ref, sem):
    pltpu.make_async_copy(ref, ref, sem).wait()


def column_of(raw, c):
    shots, ext, lanes = raw.shape
    return raw.reshape(shots * ext, lanes)[pl.ds(c, shots, stride=ext), :]


def kernel(
    n_box,
    n_shot,
    first_smem,
    sources_smem,
    wavelet_smem,
    u_prev,
    u_now,
    born_prev,
    born_now,
    adj_after,
    adj_last,
    velocity,
    receivers,
    observed,
    reflectivity,
    out,
    raw_u,
    raw_q,
    raw_b,
    raw_v,
    rec,
    obs,
    refl,
    wave_u,
    accel,
    wave_b,
    wave_q,
    grad_part,
    adj_m,
    speed,
    image,
    mask,
    target,
    tile_out,
    tile_in,
    slab_e,
    slab_l,
    stage_e,
    stage_l,
    back_e,
    back_l,
    aligned_e,
    aligned_l,
    reduce_e,
    reduce_l,
    result,
    load_sem,
    halo_send,
    halo_recv,
    box_send,
    box_recv,
    shot_send,
    shot_recv,
):
    shots, columns, depth = u_now.shape[1:]
    steps = wavelet_smem.shape[2]
    n_rec = receivers.shape[1]
    rounds = reflectivity.shape[0]
    ext = columns + 2 * HALO
    spare = rounds - n_box
    share = rounds // n_shot
    g = lax.axis_index("shot")
    p = lax.axis_index("box")
    last = n_box - 1

    barrier = pltpu.get_barrier_semaphore()

    def greet_box(k, carry):
        pl.semaphore_signal(
            barrier, inc=1, device_id={"box": lax.rem(p + k, n_box)}, device_id_type=MESH
        )
        return carry

    def greet_shot(k, carry):
        pl.semaphore_signal(
            barrier, inc=1, device_id={"shot": lax.rem(g + k, n_shot)}, device_id_type=MESH
        )
        return carry

    lax.fori_loop(1, n_box, greet_box, 0)
    lax.fori_loop(1, n_shot, greet_shot, 0)

    loads = []

    def load(src, dst):
        copy = pltpu.make_async_copy(src, dst, load_sem.at[len(loads)])
        copy.start()
        loads.append(copy)
        return copy

    half = [pl.ds(0, LANES), pl.ds(LANES, LANES)]
    own = pl.ds(HALO, columns)
    load_refl = load(reflectivity.at[:, 0, :, half[0]], refl.at[pl.ds(1, rounds)])
    load_v = [load(velocity.at[0, :, half[h]], raw_v.at[h, own]) for h in range(2)]
    load_u = [
        load(field.at[0, :, :, half[h]], raw_u.at[f, h, :, own])
        for f, field in enumerate((u_prev, u_now))
        for h in range(2)
    ]
    load_r = [load(receivers, rec.at[1]), load(observed.at[0], obs.at[1])]
    load_q = [
        load(field.at[0, :, :, half[h]], raw_q.at[f, h, :, own])
        for f, field in enumerate((adj_after, adj_last))
        for h in range(2)
    ]
    load_b = [
        load(field.at[0, :, :, half[0]], raw_b.at[f, :, own])
        for f, field in enumerate((born_prev, born_now))
    ]

    for edge, place, side in ((0, 0, 0), (last, HALO + columns, 2)):

        @pl.when(p == edge)
        def _():
            strip = pl.ds(place, HALO)
            raw_v[:, strip] = jnp.zeros((2, HALO, LANES), F32)
            raw_b[:, :, strip] = jnp.zeros((2, shots, HALO, LANES), F32)
            for f in range(2):
                raw_u[f, :, :, strip] = jnp.zeros((2, shots, HALO, LANES), F32)
                raw_q[f, :, :, strip] = jnp.zeros((2, shots, HALO, LANES), F32)
            rec[side] = jnp.full((1, n_rec), -1, jnp.int32)
            obs[side] = jnp.zeros((shots, steps, n_rec), F32)

    blank = jnp.zeros((shots, LANES), F32)
    for pad in (0, ext + 1):
        for level in range(2):
            wave_b[level, pad] = blank
            for h in range(2):
                wave_u[level, h, pad] = blank
        for level in range(wave_q.shape[0]):
            for h in range(2):
                wave_q[level, h, pad] = blank
        for level in range(steps):
            adj_m[level, pad] = blank
    for c in (0, 1, ext - 2, ext - 1):
        image[c] = blank
    refl[0] = jnp.zeros((2, LANES), F32)
    refl[rounds + 1] = jnp.zeros((2, LANES), F32)
    back_e[pl.ds(0, spare)] = jnp.zeros((spare,) + back_e.shape[1:], F32)
    back_e[pl.ds(spare + n_box, spare)] = jnp.zeros((spare,) + back_e.shape[1:], F32)
    back_l[pl.ds(0, spare)] = jnp.zeros((spare,) + back_l.shape[1:], F32)
    back_l[pl.ds(spare + n_box, spare)] = jnp.zeros((spare,) + back_l.shape[1:], F32)

    first = first_smem[0]
    rotation = lax.rem(first, n_box)
    first_round = lax.div(first, n_box) + (p < rotation).astype(jnp.int32)
    lead = lax.rem(p - first + 3 + 64 * n_box, n_box)
    source_round = lax.div(first - 3 + lead - p + 64 * n_box, n_box) - 64

    load_refl.wait()
    tile_out[:, 0] = refl[pl.ds(source_round + 1, n_box)]
    tile_out[:, 1] = refl[pl.ds(source_round + 2, n_box)]
    tile_in[p] = tile_out[p]

    pl.semaphore_wait(barrier, n_box - 1 + n_shot - 1)

    def box_exchange(staged, landing, place, sem):
        def send(k, carry):
            target_device = lax.rem(p + k, n_box)
            pltpu.make_async_remote_copy(
                src_ref=staged.at[target_device],
                dst_ref=landing.at[place],
                send_sem=box_send.at[sem],
                recv_sem=box_recv.at[sem],
                device_id={"box": target_device},
                device_id_type=MESH,
            ).start()
            return carry

        lax.fori_loop(1, n_box, send, 0)

    def box_sent(staged, sem):
        wait_bytes(staged.at[pl.ds(0, n_box - 1)], box_send.at[sem])

    def box_arrived(landing, sem):
        wait_bytes(landing.at[pl.ds(0, n_box - 1)], box_recv.at[sem])

    box_exchange(tile_out, tile_in, p, 0)

    left_edge, right_edge = pl.ds(0, HALO), pl.ds(columns - HALO, HALO)
    left_halo, right_halo = pl.ds(0, HALO), pl.ds(HALO + columns, HALO)

    def halo_pieces(edge, halo, side):
        yield 0, [
            (field.at[0, :, edge, half[h]], raw_u.at[f, h, :, halo])
            for f, field in enumerate((u_prev, u_now))
            for h in range(2)
        ]
        yield 1, [(velocity.at[0, edge, half[h]], raw_v.at[h, halo]) for h in range(2)]
        yield 2, [
            (field.at[0, :, edge, half[h]], raw_q.at[f, h, :, halo])
            for f, field in enumerate((adj_after, adj_last))
            for h in range(2)
        ]
        yield 3, [
            (field.at[0, :, edge, half[0]], raw_b.at[f, :, halo])
            for f, field in enumerate((born_prev, born_now))
        ]
        yield 4, [(receivers, rec.at[side])]
        yield 5, [(observed.at[0], obs.at[side])]

    def halo_refs(group, edge_side):
        halo = (left_halo, right_halo)[edge_side]
        side = (0, 2)[edge_side]
        return (
            raw_u.at[:, :, :, halo],
            raw_v.at[:, halo],
            raw_q.at[:, :, :, halo],
            raw_b.at[:, :, halo],
            rec.at[side],
            obs.at[side],
        )[group]

    def send_halo(direction):
        edge, halo, side = (
            (left_edge, right_halo, 2),
            (right_edge, left_halo, 0),
        )[direction]
        neighbour = (p - 1, p + 1)[direction]
        for group, pieces in halo_pieces(edge, halo, side):
            for src, dst in pieces:
                pltpu.make_async_remote_copy(
                    src_ref=src,
                    dst_ref=dst,
                    send_sem=halo_send.at[direction, group],
                    recv_sem=halo_recv.at[direction, group],
                    device_id={"box": neighbour},
                    device_id_type=MESH,
                ).start()

    @pl.when(p > 0)
    def _():
        send_halo(0)

    @pl.when(p < last)
    def _():
        send_halo(1)

    def halo_arrived(group):
        @pl.when(p < last)
        def _():
            wait_bytes(halo_refs(group, 1), halo_recv.at[0, group])

        @pl.when(p > 0)
        def _():
            wait_bytes(halo_refs(group, 0), halo_recv.at[1, group])

    def halo_sent(group):
        @pl.when(p > 0)
        def _():
            wait_bytes(halo_refs(group, 1), halo_send.at[0, group])

        @pl.when(p < last)
        def _():
            wait_bytes(halo_refs(group, 0), halo_send.at[1, group])

    lane = lax.broadcasted_iota(jnp.int32, (shots, LANES), 1)
    at_top = lane == 0
    at_bottom = lane == LANES - 1
    shot_row = lax.broadcasted_iota(jnp.int32, (shots, LANES), 0)
    first_cell = (p * columns - HALO) * depth

    def by_columns(raw, working):
        def move(c, carry):
            working[c + 1] = column_of(raw, c)
            return carry

        lax.fori_loop(0, ext, move, 0, unroll=16)

    source_cell = jnp.zeros((shots, LANES), jnp.int32)
    pulses = [jnp.zeros((shots, LANES), F32) for _ in range(steps)]
    for s in range(shots):
        source_cell = jnp.where(shot_row == s, sources_smem[0, s], source_cell)
        for t in range(steps):
            pulses[t] = jnp.where(shot_row == s, wavelet_smem[0, s, t], pulses[t])
    source_cell = source_cell - first_cell - lane

    for copy in load_u + load_v:
        copy.wait()
    halo_arrived(0)
    halo_arrived(1)
    for h in range(2):
        by_columns(raw_u.at[0, h], wave_u.at[1, h])
        by_columns(raw_u.at[1, h], wave_u.at[0, h])

        def widen(c, carry):
            speed[h, c] = jnp.broadcast_to(raw_v[h, pl.ds(c, 1), :], (shots, LANES))
            return carry

        lax.fori_loop(0, ext, widen, 0, unroll=16)

    def blocks(body, count=ext // BLOCK, offset=0):
        def step(i, carry):
            body(offset + i * BLOCK, i)
            return carry

        lax.fori_loop(0, count, step, 0, unroll=2)

    def turn(x, by):
        return pltpu.roll(x, by, axis=2)

    def lap_both(wave, level, c):
        n = [wave[level, h, pl.ds(c + 1, BLOCK)] for h in range(2)]
        down = [turn(n[h], 1) for h in range(2)]
        up = [turn(n[h], LANES - 1) for h in range(2)]
        shallow = [jnp.where(at_top, 0.0, down[0]), jnp.where(at_top, down[0], down[1])]
        deep = [jnp.where(at_bottom, up[1], up[0]), jnp.where(at_bottom, 0.0, up[1])]
        laps = [
            (wave[level, h, pl.ds(c, BLOCK)] + wave[level, h, pl.ds(c + 2, BLOCK)])
            + (shallow[h] + deep[h])
            - 4.0 * n[h]
            for h in range(2)
        ]
        return n, laps

    def lap_top(wave, level, c):
        n = wave[level, pl.ds(c + 1, BLOCK)]
        shallow = jnp.where(at_top, 0.0, turn(n, 1))
        deep = jnp.where(at_bottom, 0.0, turn(n, LANES - 1))
        lap = (wave[level, pl.ds(c, BLOCK)] + wave[level, pl.ds(c + 2, BLOCK)]) + (
            shallow + deep
        )
        return n, lap - 4.0 * n

    cell_step = lax.broadcasted_iota(jnp.int32, (BLOCK, shots, LANES), 0) * depth

    for t in range(steps):
        now, old = t % 2, 1 - t % 2

        def advance(c, i):
            n, laps = lap_both(wave_u, now, c)
            for h in range(2):
                offset = (source_cell - (c * depth + h * LANES))[None]
                a = speed[h, pl.ds(c, BLOCK)] * laps[h] + jnp.where(
                    offset == cell_step, pulses[t][None], 0.0
                )
                accel[t, h, pl.ds(c, BLOCK)] = a
                if t < steps - 1:
                    wave_u[old, h, pl.ds(c + 1, BLOCK)] = (
                        (n[h] + n[h]) - wave_u[old, h, pl.ds(c + 1, BLOCK)]
                    ) + a

        blocks(advance)

    for copy in load_q:
        copy.wait()
    halo_arrived(2)
    for h in range(2):
        by_columns(raw_q.at[0, h], wave_q.at[0, h])
        by_columns(raw_q.at[1, h], wave_q.at[1, h])
    for k in range(steps):

        def retreat(c, i):
            n, laps = lap_both(wave_q, k + 1, c)
            for h in range(2):
                wave_q[k + 2, h, pl.ds(c + 1, BLOCK)] = (
                    (n[h] + n[h]) - wave_q[k, h, pl.ds(c + 1, BLOCK)]
                ) + speed[h, pl.ds(c, BLOCK)] * laps[h]

        blocks(retreat)

    def store_rows(slab, kind, i, block):
        for r in range(BLOCK):
            row = jnp.sum(block[r], axis=0, keepdims=True)
            j = i * (BLOCK // 2) + r // 2
            slab[j, kind, pl.ds(r % 2, 1), :] = row
            slab[j + n_box, kind, pl.ds(r % 2, 1), :] = row

    def correlate(c, i):
        a = [[accel[t, h, pl.ds(c, BLOCK)] for h in range(2)] for t in range(steps)]
        q = [
            [wave_q[steps + 1 - t, h, pl.ds(c + 1, BLOCK)] for h in range(2)]
            for t in range(steps)
        ]
        for h in range(2):
            store_rows(slab_e, h, i, sum(a[t][h] * a[t][h] for t in range(steps)))
        store_rows(slab_e, 2, i, sum(q[t][1] * a[t][1] for t in range(steps)))
        grad_part[pl.ds(i * BLOCK, BLOCK)] = sum(q[t][0] * a[t][0] for t in range(steps))

    blocks(correlate, columns // BLOCK, HALO)

    turned = lax.rem(n_box - rotation, n_box)
    stage_e[...] = slab_e[pl.ds(turned, n_box)]
    back_e[spare + p] = stage_e[p]
    box_exchange(stage_e, back_e, spare + p, 1)

    for copy in load_r + load_b:
        copy.wait()
    halo_arrived(4)
    halo_arrived(5)
    halo_arrived(3)
    by_columns(raw_b.at[0], wave_b.at[1])
    by_columns(raw_b.at[1], wave_b.at[0])
    beside = HALO // 2
    heard = (
        [(0, n_rec - beside + r) for r in range(beside)]
        + [(1, r) for r in range(n_rec)]
        + [(2, r) for r in range(beside)]
    )
    cells = [rec[side] for side in range(3)]
    data = [[obs[side, :, t, :] for t in range(steps)] for side in range(3)]
    for slot, (side, r) in enumerate(heard):
        cell = jnp.broadcast_to(cells[side][:, r : r + 1], (shots, LANES)) - first_cell - lane
        amounts = [
            jnp.broadcast_to(data[side][t][:, r : r + 1], (shots, LANES))
            for t in range(steps)
        ]
        for w in range(2):
            c = 2 * slot + w
            hit = cell == c * depth
            mask[c] = jnp.where(hit, 1.0, 0.0)
            for t in range(steps):
                target[t, c] = jnp.where(hit, amounts[t], 0.0)

    box_arrived(tile_in, 0)
    for j in range(n_box + 6):
        owner = lax.rem(rotation + j - 3 + n_box, n_box)
        tile = tile_in[owner, j // n_box]
        for w in range(2):
            image[HALO - 6 + 2 * j + w] = jnp.broadcast_to(tile[w : w + 1], (shots, LANES))

    for t in range(steps):
        now, old = t % 2, 1 - t % 2

        def scatter_wave(c, i):
            n, lap = lap_top(wave_b, now, c)
            b = (
                ((n + n) - wave_b[old, pl.ds(c + 1, BLOCK)])
                + speed[0, pl.ds(c, BLOCK)] * lap
                + image[pl.ds(c, BLOCK)] * accel[t, 0, pl.ds(c, BLOCK)]
            )
            if t < steps - 1:
                wave_b[old, pl.ds(c + 1, BLOCK)] = b
            adj_m[t, pl.ds(c + 1, BLOCK)] = (
                mask[pl.ds(c, BLOCK)] * b - target[t, pl.ds(c, BLOCK)]
            )

        blocks(scatter_wave)

    for t in reversed(range(steps - 1)):

        def residual(c, i):
            n, lap = lap_top(adj_m, t + 1, c)
            q = (n + n) + speed[0, pl.ds(c, BLOCK)] * lap + adj_m[t, pl.ds(c + 1, BLOCK)]
            if t + 2 < steps:
                q = q - adj_m[t + 2, pl.ds(c + 1, BLOCK)]
            adj_m[t, pl.ds(c + 1, BLOCK)] = q

        blocks(residual)

    def correlate_late(c, i):
        total = grad_part[pl.ds(i * BLOCK, BLOCK)] + sum(
            adj_m[t, pl.ds(c + 1, BLOCK)] * accel[t, 0, pl.ds(c, BLOCK)]
            for t in range(steps)
        )
        store_rows(slab_l, 0, i, total)

    blocks(correlate_late, columns // BLOCK, HALO)
    stage_l[...] = slab_l[pl.ds(turned, n_box)]
    back_l[spare + p] = stage_l[p]
    box_exchange(stage_l, back_l, spare + p, 2)

    def shot_exchange(src_of, landing, sem):
        def send(k, carry):
            s = lax.rem(g + k, n_shot)
            pltpu.make_async_remote_copy(
                src_ref=src_of(s),
                dst_ref=landing,
                send_sem=shot_send.at[sem],
                recv_sem=shot_recv.at[sem],
                device_id={"shot": s},
                device_id_type=MESH,
            ).start()
            return carry

        lax.fori_loop(1, n_shot, send, 0)

    mine = pl.ds(g * share, share)
    others = pl.ds(0, (n_shot - 1) * share)

    def scatter_rounds(back, aligned, landing, box_sem, sem):
        box_arrived(back, box_sem)
        aligned[...] = back[pl.ds(spare - first_round, rounds)]
        landing[g] = aligned[mine]
        shot_exchange(lambda s: aligned.at[pl.ds(s * share, share)], landing.at[g], sem)

    scatter_rounds(back_e, aligned_e, reduce_e, 1, 0)
    scatter_rounds(back_l, aligned_l, reduce_l, 2, 1)
    wait_bytes(reduce_e.at[pl.ds(0, n_shot - 1)], shot_recv.at[0])
    sums = reduce_e[0]
    for s in range(1, n_shot):
        sums = sums + reduce_e[s]
    scale = [jnp.sqrt(sums[:, h] + damping) for h in range(2)]
    result[mine, 0, :, half[1]] = sums[:, 2] / scale[1]
    wait_bytes(reduce_l.at[pl.ds(0, n_shot - 1)], shot_recv.at[1])
    sums = reduce_l[0, :, 0]
    for s in range(1, n_shot):
        sums = sums + reduce_l[s, :, 0]
    result[mine, 0, :, half[0]] = sums / scale[0]
    shot_exchange(lambda s: result.at[mine], result.at[mine], 2)
    wait_bytes(result.at[others], shot_recv.at[2])
    pltpu.sync_copy(result, out)

    for group in range(6):
        halo_sent(group)
    box_sent(tile_out, 0)
    box_sent(stage_e, 1)
    box_sent(stage_l, 2)
    wait_bytes(aligned_e.at[others], shot_send.at[0])
    wait_bytes(aligned_l.at[others], shot_send.at[1])
    wait_bytes(result.at[others], shot_send.at[2])


def on_device(
    n_box,
    n_shot,
    u_prev,
    u_now,
    born_prev,
    born_now,
    adj_after,
    adj_last,
    velocity,
    wavelet,
    sources,
    receivers,
    observed,
    first_tile,
    reflectivity,
):
    shots, columns, depth = u_now.shape[1:]
    steps = wavelet.shape[2]
    n_rec = receivers.shape[1]
    rounds = reflectivity.shape[0]
    ext = columns + 2 * HALO
    spare = rounds - n_box
    share = rounds // n_shot

    def vmem(*dims):
        return pltpu.VMEM(dims, F32)

    plane = (shots, LANES)
    tile = (2, LANES)
    scratch = [
        vmem(2, 2, shots, ext, LANES),
        vmem(2, 2, shots, ext, LANES),
        vmem(2, shots, ext, LANES),
        vmem(2, ext, LANES),
        pltpu.VMEM((3, 1, n_rec), jnp.int32),
        vmem(3, shots, steps, n_rec),
        vmem(rounds + 2, *tile),
        vmem(2, 2, ext + 2, *plane),
        vmem(steps, 2, ext, *plane),
        vmem(2, ext + 2, *plane),
        vmem(steps + 2, 2, ext + 2, *plane),
        vmem(columns, *plane),
        vmem(steps, ext + 2, *plane),
        vmem(2, ext, *plane),
        vmem(ext, *plane),
        vmem(ext, *plane),
        vmem(steps, ext, *plane),
        vmem(n_box, 2, *tile),
        vmem(n_box, 2, *tile),
        vmem(2 * n_box, 3, *tile),
        vmem(2 * n_box, 1, *tile),
        vmem(n_box, 3, *tile),
        vmem(n_box, 1, *tile),
        vmem(n_box + 2 * spare, 3, *tile),
        vmem(n_box + 2 * spare, 1, *tile),
        vmem(rounds, 3, *tile),
        vmem(rounds, 1, *tile),
        vmem(n_shot, share, 3, *tile),
        vmem(n_shot, share, 1, *tile),
        vmem(rounds, 1, 2, depth),
        pltpu.SemaphoreType.DMA((17,)),
        pltpu.SemaphoreType.DMA((2, 6)),
        pltpu.SemaphoreType.DMA((2, 6)),
        pltpu.SemaphoreType.DMA((3,)),
        pltpu.SemaphoreType.DMA((3,)),
        pltpu.SemaphoreType.DMA((3,)),
        pltpu.SemaphoreType.DMA((3,)),
    ]
    smem = pl.BlockSpec(memory_space=pltpu.SMEM)
    anywhere = pl.BlockSpec(memory_space=pl.ANY)
    return pl.pallas_call(
        functools.partial(kernel, n_box, n_shot),
        out_shape=jax.ShapeDtypeStruct(reflectivity.shape, F32),
        in_specs=[smem] * 3 + [anywhere] * 10,
        out_specs=anywhere,
        scratch_shapes=scratch,
        compiler_params=pltpu.CompilerParams(
            collective_id=0, has_side_effects=True, vmem_limit_bytes=48 * 1024 * 1024
        ),
    )(
        first_tile,
        sources,
        wavelet,
        u_prev,
        u_now,
        born_prev,
        born_now,
        adj_after,
        adj_last,
        velocity,
        receivers,
        observed,
        reflectivity,
    )


def solution(mesh):
    return jax.shard_map(
        functools.partial(on_device, mesh.shape["box"], mesh.shape["shot"]),
        mesh=mesh,
        in_specs=(
            P("shot", None, "box", None),
            P("shot", None, "box", None),
            P("shot", None, "box", None),
            P("shot", None, "box", None),
            P("shot", None, "box", None),
            P("shot", None, "box", None),
            P("shot", "box", None),
            P("shot", None, None),
            P("shot", None),
            P("shot", "box"),
            P("shot", None, None, "box"),
            P("shot"),
            P(None, "box", None, None),
        ),
        out_specs=P(None, "box", None, None),
        check_vma=False,
    )
```

time: 326 us -> 55.1 us (0.17); the launches traced: 320 us -> 54.4 us
  waiting for transfers between devices: 96.1 us -> 0 us
  starting transfers between devices: 85.2 us -> 0 us
  local copies, waits for them, and re-layouts: 69.8 us -> 10.1 us
  other arithmetic: 54.4 us -> 0 us
  Pallas kernels: 0 us -> 43.6 us
  between operations: 14.9 us -> 0.69 us
    psum x1 -> x0, waiting for transfers between devices: 78.6 us -> none  [on_device(): total_grad, total_illum = lax.psum((grad_rounds, illum_rounds), 'shot')]
    ppermute x16 -> x0, starting transfers between devices: 46 us -> none  [the longest x8 30.4 us: padded_2(): lax.ppermute(lax.slice_in_dim(block, block.shape[dim] - width, None, axis...]
    pallas_call x0 -> x1, Pallas kernels: none -> 43.6 us  [on_device(): pl.pallas_call(functools.partial(kernel, n_box, n_shot), out_shape=jax.Sh...]
    all_to_all x3 -> x0, starting transfers between devices: 39.2 us -> none  [the longest x1 23.4 us: on_device(): lax.all_to_all(to_owner(illumination), 'box', split_axis=0, concat_axis=0...]
    add x10 -> x0, local copies, waits for them, and re-layouts: 38 us -> none  [the longest x4 19.6 us: on_device(): 2.0 * newer_b - older_b + speed_slab * lap_all[shot_count:]]
    scatter-add x4 -> x0, local copies, waits for them, and re-layouts: 20.6 us -> none  [on_device(): adjoint_next.at[:, receiver_column, receiver_depth].add(misfit)]
    scatter-add x8 -> x0, other arithmetic: 18.6 us -> none  [the longest x4 14.9 us: on_device(): adjoint_next.at[:, receiver_column, receiver_depth].add(misfit)]
    all_to_all x3 -> x0, waiting for transfers between devices: 15.3 us -> none  [the longest x1 8.06 us: on_device(): lax.all_to_all(to_owner(gradient), 'box', split_axis=0, concat_axis=0, ti...]
  transfers between devices with their start and end apart: 20 -> 0, of which waited for: 6 -> 0; matrix products, arithmetic and copies ran while one was open for 16% -> 0% of each run, Pallas kernels for 0% -> 0%
where the time goes in v1:
time: 55.1 us; the launch traced here: 54.4 us
  Pallas kernels  43.6 us (79%)
  local copies, waits for them, and re-layouts  10.1 us (18%)
  between operations  0.69 us (1%)
    pallas_call x1, Pallas kernels, on_device(): pl.pallas_call(functools.partial(kernel, n_box, n_shot), out_shape=jax.Sh...  43.6 us
    unnamed x24, local copies, waits for them, and re-layouts  10.1 us

profile of v1, /device:TPU:1, one launch (start us, length us, event | category | flops | bytes accessed | tf_op | source)
XLA Modules:
  0.0 54.4 jit_solution(4042496241801641051)
XLA Ops:
  0.7 0.0 copy-start.9
  0.7 0.0 copy-start.10
  0.7 0.8 %copy.14.wavelet_smem = f32[1,8,4]{2,1,0:T(8,128)S(1)} copy(f32[1,8,4]{1,2,0:T(4,128)} %param.20) | data formatting | bytes 256 | tf_op args[7]
  1.4 0.0 copy-done.9
  1.4 0.0 copy-done.10
  1.4 0.0 copy-start
  1.4 1.0 %copy-done = f32[1,8,64,256]{3,2,1,0:T(8,128)S(1)} copy-done((f32[1,8,64,256]{3,2,1,0:T(8,128)S(1)}, f32[1,8,64,256]{3,2,1,0:T(8,128)}, u32[]{:S(2)}) %copy-start) | copy-done | bytes 524312
  2.5 0.0 copy-start.1
  2.5 1.0 %copy-done.1 = f32[1,8,64,256]{3,2,1,0:T(8,128)S(1)} copy-done((f32[1,8,64,256]{3,2,1,0:T(8,128)S(1)}, f32[1,8,64,256]{3,2,1,0:T(8,128)}, u32[]{:S(2)}) %copy-start.1) | copy-done | bytes 524312
  3.5 0.0 copy-start.2
  3.5 1.0 %copy-done.2 = f32[1,8,64,256]{3,2,1,0:T(8,128)S(1)} copy-done((f32[1,8,64,256]{3,2,1,0:T(8,128)S(1)}, f32[1,8,64,256]{3,2,1,0:T(8,128)}, u32[]{:S(2)}) %copy-start.2) | copy-done | bytes 524312
  4.6 0.0 copy-start.3
  4.6 1.0 %copy-done.3 = f32[1,8,64,256]{3,2,1,0:T(8,128)S(1)} copy-done((f32[1,8,64,256]{3,2,1,0:T(8,128)S(1)}, f32[1,8,64,256]{3,2,1,0:T(8,128)}, u32[]{:S(2)}) %copy-start.3) | copy-done | bytes 524312
  5.6 0.0 copy-start.4
  5.6 1.0 %copy-done.4 = f32[1,8,64,256]{3,2,1,0:T(8,128)S(1)} copy-done((f32[1,8,64,256]{3,2,1,0:T(8,128)S(1)}, f32[1,8,64,256]{3,2,1,0:T(8,128)}, u32[]{:S(2)}) %copy-start.4) | copy-done | bytes 524312
  6.7 0.0 copy-start.5
  6.7 1.0 %copy-done.5 = f32[1,8,64,256]{3,2,1,0:T(8,128)S(1)} copy-done((f32[1,8,64,256]{3,2,1,0:T(8,128)S(1)}, f32[1,8,64,256]{3,2,1,0:T(8,128)}, u32[]{:S(2)}) %copy-start.5) | copy-done | bytes 524312
  7.7 0.0 copy-start.6
  7.7 0.9 %copy-done.6 = f32[40,1,2,256]{3,2,1,0:T(2,128)S(1)} copy-done((f32[40,1,2,256]{3,2,1,0:T(2,128)S(1)}, f32[40,1,2,256]{3,2,1,0:T(2,128)}, u32[]{:S(2)}) %copy-start.6) | copy-done | bytes 81944
  8.6 0.0 copy-start.7
  8.6 0.8 %copy-done.7 = f32[1,64,256]{2,1,0:T(8,128)S(1)} copy-done((f32[1,64,256]{2,1,0:T(8,128)S(1)}, f32[1,64,256]{2,1,0:T(8,128)}, u32[]{:S(2)}) %copy-start.7) | copy-done | bytes 65560
  9.4 0.0 copy-start.8
  9.4 0.7 %copy-done.8 = f32[1,8,4,32]{3,2,1,0:T(4,128)S(1)} copy-done((f32[1,8,4,32]{3,2,1,0:T(4,128)S(1)}, f32[1,8,4,32]{3,2,1,0:T(4,128)}, u32[]{:S(2)}) %copy-start.8) | copy-done | bytes 4120
  10.1 43.6 %shard_map.127 = f32[40,1,2,256]{3,2,1,0:T(2,128)S(1)} custom-call(s32[1]{0:T(128)S(6)} %copy.16.first_smem, s32[1,8]{1,0:T(1,128)S(1)} %copy-done.9, f32[1,8,4]{2,1,0:T(8,128)S(1)} %copy.14.wavelet_smem, f32[1,8,64,256]{3,2,1,0:T(8,128)S(1)} %copy-done, f32[1,8,64,256]{3,2,1,0:T(8,128)S(1)} %copy-done.1, f32[1,8,64,256]{3,2,1,0:T(8,128)S(1)} %copy-done.2, ...), custom_call_target="tpu_custom_call" | custom-call | tf_op jit(solution)/shard_map/pallas_call | solution.py:612
  53.8 0.6 %copy.17 = f32[40,1,2,256]{3,2,1,0:T(2,128)} copy(f32[40,1,2,256]{3,2,1,0:T(2,128)S(1)} %shard_map.127) | data formatting | bytes 163840
Async XLA Ops:
  0.7 0.8 %copy-start.9 = (s32[1,8]{1,0:T(1,128)S(1)}, s32[1,8]{1,0:T(1,128)}, u32[]{:S(2)}) copy-start(s32[1,8]{1,0:T(1,128)} %sources_smem.1) | copy-start | bytes 100
  0.7 0.8 %copy-start.10 = (s32[1,32]{1,0:T(1,128)S(1)}, s32[1,32]{1,0:T(1,128)}, u32[]{:S(2)}) copy-start(s32[1,32]{1,0:T(1,128)} %receivers.1) | copy-start | bytes 388
  1.4 1.0 %copy-start = (f32[1,8,64,256]{3,2,1,0:T(8,128)S(1)}, f32[1,8,64,256]{3,2,1,0:T(8,128)}, u32[]{:S(2)}) copy-start(f32[1,8,64,256]{3,2,1,0:T(8,128)} %u_prev.1) | copy-start | bytes 1572868
  2.5 1.0 %copy-start.1 = (f32[1,8,64,256]{3,2,1,0:T(8,128)S(1)}, f32[1,8,64,256]{3,2,1,0:T(8,128)}, u32[]{:S(2)}) copy-start(f32[1,8,64,256]{3,2,1,0:T(8,128)} %u_now.1) | copy-start | bytes 1572868
  3.5 1.0 %copy-start.2 = (f32[1,8,64,256]{3,2,1,0:T(8,128)S(1)}, f32[1,8,64,256]{3,2,1,0:T(8,128)}, u32[]{:S(2)}) copy-start(f32[1,8,64,256]{3,2,1,0:T(8,128)} %born_prev.1) | copy-start | bytes 1572868
  4.6 1.0 %copy-start.3 = (f32[1,8,64,256]{3,2,1,0:T(8,128)S(1)}, f32[1,8,64,256]{3,2,1,0:T(8,128)}, u32[]{:S(2)}) copy-start(f32[1,8,64,256]{3,2,1,0:T(8,128)} %born_now.1) | copy-start | bytes 1572868
  5.6 1.0 %copy-start.4 = (f32[1,8,64,256]{3,2,1,0:T(8,128)S(1)}, f32[1,8,64,256]{3,2,1,0:T(8,128)}, u32[]{:S(2)}) copy-start(f32[1,8,64,256]{3,2,1,0:T(8,128)} %adj_after.1) | copy-start | bytes 1572868
  6.7 1.0 %copy-start.5 = (f32[1,8,64,256]{3,2,1,0:T(8,128)S(1)}, f32[1,8,64,256]{3,2,1,0:T(8,128)}, u32[]{:S(2)}) copy-start(f32[1,8,64,256]{3,2,1,0:T(8,128)} %adj_last.1) | copy-start | bytes 1572868
  7.7 0.9 %copy-start.6 = (f32[40,1,2,256]{3,2,1,0:T(2,128)S(1)}, f32[40,1,2,256]{3,2,1,0:T(2,128)}, u32[]{:S(2)}) copy-start(f32[40,1,2,256]{3,2,1,0:T(2,128)} %reflectivity.1) | copy-start | bytes 245764
  8.6 0.8 %copy-start.7 = (f32[1,64,256]{2,1,0:T(8,128)S(1)}, f32[1,64,256]{2,1,0:T(8,128)}, u32[]{:S(2)}) copy-start(f32[1,64,256]{2,1,0:T(8,128)} %velocity.1) | copy-start | bytes 196612
  9.4 0.7 %copy-start.8 = (f32[1,8,4,32]{3,2,1,0:T(4,128)S(1)}, f32[1,8,4,32]{3,2,1,0:T(4,128)}, u32[]{:S(2)}) copy-start(f32[1,8,4,32]{3,2,1,0:T(4,128)} %observed.1) | copy-start | bytes 12292

commit v2 on v1

--- a/solution.py
+++ b/solution.py
@@ -27,9 +27,9 @@
 def kernel(
     n_box,
     n_shot,
-    first_smem,
-    sources_smem,
-    wavelet_smem,
+    first_tile,
+    sources,
+    wavelet,
     u_prev,
     u_now,
     born_prev,
@@ -41,6 +41,8 @@
     observed,
     reflectivity,
     out,
+    sources_smem,
+    wavelet_smem,
     raw_u,
     raw_q,
     raw_b,
@@ -80,7 +82,7 @@
     shot_recv,
 ):
     shots, columns, depth = u_now.shape[1:]
-    steps = wavelet_smem.shape[2]
+    steps = wavelet_smem.shape[1]
     n_rec = receivers.shape[1]
     rounds = reflectivity.shape[0]
     ext = columns + 2 * HALO
@@ -124,6 +126,7 @@
         for f, field in enumerate((u_prev, u_now))
         for h in range(2)
     ]
+    load_s = [load(sources, sources_smem), load(wavelet, wavelet_smem)]
     load_r = [load(receivers, rec.at[1]), load(observed.at[0], obs.at[1])]
     load_q = [
         load(field.at[0, :, :, half[h]], raw_q.at[f, h, :, own])
@@ -168,7 +171,7 @@
     back_l[pl.ds(0, spare)] = jnp.zeros((spare,) + back_l.shape[1:], F32)
     back_l[pl.ds(spare + n_box, spare)] = jnp.zeros((spare,) + back_l.shape[1:], F32)
 
-    first = first_smem[0]
+    first = first_tile[0]
     rotation = lax.rem(first, n_box)
     first_round = lax.div(first, n_box) + (p < rotation).astype(jnp.int32)
     lead = lax.rem(p - first + 3 + 64 * n_box, n_box)
@@ -294,12 +297,14 @@
 
         lax.fori_loop(0, ext, move, 0, unroll=16)
 
+    for copy in load_s:
+        copy.wait()
     source_cell = jnp.zeros((shots, LANES), jnp.int32)
     pulses = [jnp.zeros((shots, LANES), F32) for _ in range(steps)]
     for s in range(shots):
         source_cell = jnp.where(shot_row == s, sources_smem[0, s], source_cell)
         for t in range(steps):
-            pulses[t] = jnp.where(shot_row == s, wavelet_smem[0, s, t], pulses[t])
+            pulses[t] = jnp.where(shot_row == s, wavelet_smem[0, t, s], pulses[t])
     source_cell = source_cell - first_cell - lane
 
     for copy in load_u + load_v:
@@ -569,6 +574,8 @@
     plane = (shots, LANES)
     tile = (2, LANES)
     scratch = [
+        pltpu.SMEM(sources.shape, jnp.int32),
+        pltpu.SMEM((1, steps, shots), F32),
         vmem(2, 2, shots, ext, LANES),
         vmem(2, 2, shots, ext, LANES),
         vmem(2, shots, ext, LANES),
@@ -599,7 +606,7 @@
         vmem(n_shot, share, 3, *tile),
         vmem(n_shot, share, 1, *tile),
         vmem(rounds, 1, 2, depth),
-        pltpu.SemaphoreType.DMA((17,)),
+        pltpu.SemaphoreType.DMA((19,)),
         pltpu.SemaphoreType.DMA((2, 6)),
         pltpu.SemaphoreType.DMA((2, 6)),
         pltpu.SemaphoreType.DMA((3,)),
@@ -607,21 +614,20 @@
         pltpu.SemaphoreType.DMA((3,)),
         pltpu.SemaphoreType.DMA((3,)),
     ]
-    smem = pl.BlockSpec(memory_space=pltpu.SMEM)
-    anywhere = pl.BlockSpec(memory_space=pl.ANY)
+    hbm = pl.BlockSpec(memory_space=pltpu.HBM)
     return pl.pallas_call(
         functools.partial(kernel, n_box, n_shot),
         out_shape=jax.ShapeDtypeStruct(reflectivity.shape, F32),
-        in_specs=[smem] * 3 + [anywhere] * 10,
-        out_specs=anywhere,
+        in_specs=[pl.BlockSpec(memory_space=pltpu.SMEM)] + [hbm] * 12,
+        out_specs=hbm,
         scratch_shapes=scratch,
         compiler_params=pltpu.CompilerParams(
-            collective_id=0, has_side_effects=True, vmem_limit_bytes=48 * 1024 * 1024
+            collective_id=0, has_side_effects=True, vmem_limit_bytes=67043328
         ),
     )(
         first_tile,
         sources,
-        wavelet,
+        jnp.transpose(wavelet, (0, 2, 1)),
         u_prev,
         u_now,
         born_prev,

time: 55.1 us -> 46.4 us (0.84)
  local copies, waits for them, and re-layouts: 10.1 us -> 1.53 us
    unnamed x24 -> x1, local copies, waits for them, and re-layouts: 10.1 us -> 1.53 us
where the time goes in v2:
time: 46.4 us; the launch traced here: 46.2 us
  Pallas kernels  44 us (95%)
  local copies, waits for them, and re-layouts  1.53 us (3%)
  between operations  0.66 us (1%)
    pallas_call x1, Pallas kernels, on_device(): pl.pallas_call(functools.partial(kernel, n_box, n_shot), out_shape=jax.Sh...  44 us
    unnamed x1, local copies, waits for them, and re-layouts  1.53 us

profile of v2, /device:TPU:1, one launch (start us, length us, event | category | flops | bytes accessed | tf_op | source)
XLA Modules:
  0.0 46.2 jit_solution(4569936644229581342)
XLA Ops:
  0.7 44.0 %shard_map.127 = f32[40,1,2,256]{3,2,1,0:T(2,128)} custom-call(s32[1]{0:T(128)S(6)} %copy.15.first_tile, s32[1,8]{1,0:T(1,128)} %sources.1, f32[1,4,8]{2,1,0:T(4,128)} %bitcast.1, f32[1,8,64,256]{3,2,1,0:T(8,128)} %u_prev.1, f32[1,8,64,256]{3,2,1,0:T(8,128)} %u_now.1, f32[1,8,64,256]{3,2,1,0:T(8,128)} %born_prev.1, f32[1,8,64,256]{3,2,1,0:T(8,128)} %born_now.1, ...), custom_call_target="tpu_custom_call" | custom-call | tf_op jit(solution)/shard_map/pallas_call | solution.py:618
  44.7 1.5 %copy.16 = f32[40,1,2,256]{3,2,1,0:T(2,128)} copy(f32[40,1,2,256]{3,2,1,0:T(2,128)} %shard_map.127) | data formatting | bytes 163840

commit v3 on v2

v3 whole, which is shorter than its diff:
```python
import functools

import jax
import jax.numpy as jnp
from jax import lax
from jax.experimental import pallas as pl
from jax.experimental.pallas import tpu as pltpu
from jax.sharding import PartitionSpec as P

damping = 1.0
LANES = 128
HALO = 8
BLOCK = 8
F32 = jnp.float32
MESH = pl.DeviceIdType.MESH


def wait_bytes(ref, sem):
    pltpu.make_async_copy(ref, ref, sem).wait()


def column_of(raw, c):
    shots, ext, lanes = raw.shape
    return raw.reshape(shots * ext, lanes)[pl.ds(c, shots, stride=ext), :]


def kernel(
    n_box,
    n_shot,
    first_tile,
    sources,
    wavelet,
    u_prev,
    u_now,
    born_prev,
    born_now,
    adj_after,
    adj_last,
    velocity,
    receivers,
    observed,
    reflectivity,
    out,
    sources_smem,
    wavelet_smem,
    raw_u,
    raw_q,
    raw_b,
    raw_v,
    rec,
    obs,
    refl,
    wave_u,
    accel,
    wave_b,
    wave_q,
    grad_part,
    adj_m,
    speed,
    image,
    mask,
    target,
    by_step,
    adj_r,
    tile_out,
    tile_in,
    slab_i,
    slab_d,
    slab_s,
    stage_i,
    stage_d,
    stage_s,
    back_i,
    back_d,
    back_s,
    aligned_i,
    aligned_d,
    aligned_s,
    reduce_i,
    gather_d,
    gather_s,
    scale,
    load_sem,
    halo_send,
    halo_recv,
    box_send,
    box_recv,
    shot_send,
    shot_recv,
):
    shots, columns, depth = u_now.shape[1:]
    steps = wavelet_smem.shape[1]
    n_rec = receivers.shape[1]
    rounds = reflectivity.shape[0]
    ext = columns + 2 * HALO
    spare = rounds - n_box
    share = rounds // n_shot
    g = lax.axis_index("shot")
    p = lax.axis_index("box")
    last = n_box - 1

    barrier = pltpu.get_barrier_semaphore()

    def greet_box(k, carry):
        pl.semaphore_signal(
            barrier, inc=1, device_id={"box": lax.rem(p + k, n_box)}, device_id_type=MESH
        )
        return carry

    def greet_shot(k, carry):
        pl.semaphore_signal(
            barrier, inc=1, device_id={"shot": lax.rem(g + k, n_shot)}, device_id_type=MESH
        )
        return carry

    lax.fori_loop(1, n_box, greet_box, 0)
    lax.fori_loop(1, n_shot, greet_shot, 0)

    loads = []

    def load(src, dst):
        copy = pltpu.make_async_copy(src, dst, load_sem.at[len(loads)])
        copy.start()
        loads.append(copy)
        return copy

    half = [pl.ds(0, LANES), pl.ds(LANES, LANES)]
    own = pl.ds(HALO, columns)
    load_refl = load(reflectivity.at[:, 0, :, half[0]], refl.at[pl.ds(1, rounds)])
    load_v = [load(velocity.at[0, :, half[h]], raw_v.at[h, own]) for h in range(2)]
    load_u = [
        load(field.at[0, :, :, half[h]], raw_u.at[f, h, :, own])
        for f, field in enumerate((u_prev, u_now))
        for h in range(2)
    ]
    load_s = [load(sources, sources_smem), load(wavelet, wavelet_smem)]
    load_r = [load(receivers, rec.at[1]), load(observed.at[0], obs.at[1])]
    load_q = [
        load(field.at[0, :, :, half[h]], raw_q.at[f, h, :, own])
        for f, field in enumerate((adj_after, adj_last))
        for h in range(2)
    ]
    load_b = [
        load(field.at[0, :, :, half[0]], raw_b.at[f, :, own])
        for f, field in enumerate((born_prev, born_now))
    ]

    for edge, place, side in ((0, 0, 0), (last, HALO + columns, 2)):

        @pl.when(p == edge)
        def _():
            strip = pl.ds(place, HALO)
            raw_v[:, strip] = jnp.zeros((2, HALO, LANES), F32)
            raw_b[:, :, strip] = jnp.zeros((2, shots, HALO, LANES), F32)
            for f in range(2):
                raw_u[f, :, :, strip] = jnp.zeros((2, shots, HALO, LANES), F32)
                raw_q[f, :, :, strip] = jnp.zeros((2, shots, HALO, LANES), F32)
            rec[side] = jnp.full((1, n_rec), -1, jnp.int32)
            obs[side] = jnp.zeros((shots, steps, n_rec), F32)

    refl[0] = jnp.zeros((2, LANES), F32)
    refl[rounds + 1] = jnp.zeros((2, LANES), F32)

    first = first_tile[0]
    rotation = lax.rem(first, n_box)
    first_round = lax.div(first, n_box) + (p < rotation).astype(jnp.int32)
    lead = lax.rem(p - first + 3 + 64 * n_box, n_box)
    source_round = lax.div(first - 3 + lead - p + 64 * n_box, n_box) - 64

    load_refl.wait()
    tile_out[:, 0] = refl[pl.ds(source_round + 1, n_box)]
    tile_out[:, 1] = refl[pl.ds(source_round + 2, n_box)]
    tile_in[p] = tile_out[p]

    pl.semaphore_wait(barrier, n_box - 1 + n_shot - 1)

    def box_exchange(staged, landing, place, sem):
        def send(k, carry):
            target_device = lax.rem(p + k, n_box)
            pltpu.make_async_remote_copy(
                src_ref=staged.at[target_device],
                dst_ref=landing.at[place],
                send_sem=box_send.at[sem],
                recv_sem=box_recv.at[sem],
                device_id={"box": target_device},
                device_id_type=MESH,
            ).start()
            return carry

        lax.fori_loop(1, n_box, send, 0)

    def box_sent(staged, sem):
        wait_bytes(staged.at[pl.ds(0, n_box - 1)], box_send.at[sem])

    def box_arrived(landing, sem):
        wait_bytes(landing.at[pl.ds(0, n_box - 1)], box_recv.at[sem])

    left_edge, right_edge = pl.ds(0, HALO), pl.ds(columns - HALO, HALO)
    left_halo, right_halo = pl.ds(0, HALO), pl.ds(HALO + columns, HALO)

    def halo_pieces(edge, halo, side):
        yield 0, [
            (field.at[0, :, edge, half[h]], raw_u.at[f, h, :, halo])
            for f, field in enumerate((u_prev, u_now))
            for h in range(2)
        ]
        yield 1, [(velocity.at[0, edge, half[h]], raw_v.at[h, halo]) for h in range(2)]
        yield 2, [
            (field.at[0, :, edge, half[h]], raw_q.at[f, h, :, halo])
            for f, field in enumerate((adj_after, adj_last))
            for h in range(2)
        ]
        yield 3, [
            (field.at[0, :, edge, half[0]], raw_b.at[f, :, halo])
            for f, field in enumerate((born_prev, born_now))
        ]
        yield 4, [(receivers, rec.at[side])]
        yield 5, [(observed.at[0], obs.at[side])]

    def halo_refs(group, edge_side):
        halo = (left_halo, right_halo)[edge_side]
        side = (0, 2)[edge_side]
        return (
            raw_u.at[:, :, :, halo],
            raw_v.at[:, halo],
            raw_q.at[:, :, :, halo],
            raw_b.at[:, :, halo],
            rec.at[side],
            obs.at[side],
        )[group]

    def send_halo(direction, groups):
        edge, halo, side = (
            (left_edge, right_halo, 2),
            (right_edge, left_halo, 0),
        )[direction]
        neighbour = (p - 1, p + 1)[direction]
        for group, pieces in halo_pieces(edge, halo, side):
            if group not in groups:
                continue
            for src, dst in pieces:
                pltpu.make_async_remote_copy(
                    src_ref=src,
                    dst_ref=dst,
                    send_sem=halo_send.at[direction, group],
                    recv_sem=halo_recv.at[direction, group],
                    device_id={"box": neighbour},
                    device_id_type=MESH,
                ).start()

    def send_halos(groups):
        @pl.when(p > 0)
        def _():
            send_halo(0, groups)

        @pl.when(p < last)
        def _():
            send_halo(1, groups)

    send_halos((0, 1))
    box_exchange(tile_out, tile_in, p, 0)
    send_halos((2, 3, 4, 5))

    blank = jnp.zeros((shots, LANES), F32)
    for pad in (0, ext + 1):
        for level in range(2):
            wave_b[level, pad] = blank
        for level in range(steps):
            adj_m[level, pad] = blank
    for c in (0, 1, ext - 2, ext - 1):
        image[c] = blank
    for back in (back_i, back_d, back_s):
        for place in (0, spare + n_box):
            back[pl.ds(place, spare)] = jnp.zeros((spare,) + back.shape[1:], F32)

    def halo_arrived(group):
        @pl.when(p < last)
        def _():
            wait_bytes(halo_refs(group, 1), halo_recv.at[0, group])

        @pl.when(p > 0)
        def _():
            wait_bytes(halo_refs(group, 0), halo_recv.at[1, group])

    def halo_sent(group):
        @pl.when(p > 0)
        def _():
            wait_bytes(halo_refs(group, 1), halo_send.at[0, group])

        @pl.when(p < last)
        def _():
            wait_bytes(halo_refs(group, 0), halo_send.at[1, group])

    lane = lax.broadcasted_iota(jnp.int32, (shots, LANES), 1)
    at_top = lane == 0
    at_bottom = lane == LANES - 1
    shot_row = lax.broadcasted_iota(jnp.int32, (shots, LANES), 0)
    first_cell = (p * columns - HALO) * depth

    def by_columns(raw, working, start, count):
        def move(c, carry):
            working[start + c + 1] = column_of(raw, start + c)
            return carry

        lax.fori_loop(0, count, move, 0, unroll=min(count, 16))

    def widen(start, count):
        for h in range(2):

            def spread(c, carry):
                speed[h, start + c] = jnp.broadcast_to(
                    raw_v[h, pl.ds(start + c, 1), :], (shots, LANES)
                )
                return carry

            lax.fori_loop(0, count, spread, 0, unroll=min(count, 16))

    for copy in load_s:
        copy.wait()
    source_cell = jnp.zeros((shots, LANES), jnp.int32)
    pulses = [jnp.zeros((shots, LANES), F32) for _ in range(steps)]
    for s in range(shots):
        source_cell = jnp.where(shot_row == s, sources_smem[0, s], source_cell)
        for t in range(steps):
            pulses[t] = jnp.where(shot_row == s, wavelet_smem[0, t, s], pulses[t])
    source_cell = source_cell - first_cell - lane

    def blocks(body, start, stop, unroll):
        count = -(-(stop - start) // BLOCK)

        def step(i, carry):
            body(jnp.minimum(start + i * BLOCK, stop - BLOCK), i)
            return carry

        lax.fori_loop(0, count, step, 0, unroll=unroll if count % unroll == 0 else 1)

    def turn(x, by):
        return pltpu.roll(x, by, axis=2)

    def around(wave, c):
        wide = wave[pl.ds(c, BLOCK + 2)]
        return wide[1 : BLOCK + 1], wide[:BLOCK] + wide[2:]

    def lap_both(wave, level, c):
        pairs = [around(wave.at[level, h], c) for h in range(2)]
        n = [pair[0] for pair in pairs]
        down = [turn(n[h], 1) for h in range(2)]
        up = [turn(n[h], LANES - 1) for h in range(2)]
        shallow = [jnp.where(at_top, 0.0, down[0]), jnp.where(at_top, down[0], down[1])]
        deep = [jnp.where(at_bottom, up[1], up[0]), jnp.where(at_bottom, 0.0, up[1])]
        laps = [pairs[h][1] + (shallow[h] + deep[h]) - 4.0 * n[h] for h in range(2)]
        return n, laps

    def lap_top(wave, level, c, closed):
        n, sides = around(wave.at[level], c)
        shallow = jnp.where(at_top, 0.0, turn(n, 1))
        deep = turn(n, LANES - 1)
        if closed:
            deep = jnp.where(at_bottom, 0.0, deep)
        return n, sides + (shallow + deep) - 4.0 * n

    def store_rows(slab, kind, i, block):
        for r in range(BLOCK):
            row = jnp.sum(block[r], axis=0, keepdims=True)
            j = i * (BLOCK // 2) + r // 2
            slab[j, kind, pl.ds(r % 2, 1), :] = row
            slab[j + n_box, kind, pl.ds(r % 2, 1), :] = row

    turned = lax.rem(n_box - rotation, n_box)

    def to_owners(slab, staged, back, sem):
        staged[...] = slab[pl.ds(turned, n_box)]
        back[spare + p] = staged[p]
        box_exchange(staged, back, spare + p, sem)

    def from_boxes(back, aligned, sem):
        box_arrived(back, sem)
        aligned[...] = back[pl.ds(spare - first_round, rounds)]

    def shot_exchange(src_of, landing, sem):
        def send(k, carry):
            s = lax.rem(g + k, n_shot)
            pltpu.make_async_remote_copy(
                src_ref=src_of(s),
                dst_ref=landing,
                send_sem=shot_send.at[sem],
                recv_sem=shot_recv.at[sem],
                device_id={"shot": s},
                device_id_type=MESH,
            ).start()
            return carry

        lax.fori_loop(1, n_shot, send, 0)

    def to_all(aligned, gathered, sem):
        shot_exchange(lambda s: aligned, gathered.at[g], sem)
        gathered[g] = aligned[...]

    mine = pl.ds(g * share, share)
    others = pl.ds(0, (n_shot - 1) * share)
    cell_step = lax.broadcasted_iota(jnp.int32, (BLOCK, shots, LANES), 0) * depth

    def advance(t, c):
        n, laps = lap_both(wave_u, t + 1, c)
        for h in range(2):
            offset = (source_cell - (c * depth + h * LANES))[None]
            a = speed[h, pl.ds(c, BLOCK)] * laps[h] + jnp.where(
                offset == cell_step, pulses[t][None], 0.0
            )
            accel[t, h, pl.ds(c, BLOCK)] = a
            if t < steps - 1:
                wave_u[t + 2, h, pl.ds(c + 1, BLOCK)] = (
                    (n[h] + n[h]) - wave_u[t, h, pl.ds(c + 1, BLOCK)]
                ) + a

    for copy in load_u + load_v:
        copy.wait()
    widen(HALO, columns)
    for h in range(2):
        for level in range(2):
            by_columns(raw_u.at[level, h], wave_u.at[level, h], HALO, columns)
    for t in range(steps):
        blocks(lambda c, i: advance(t, c), HALO + 1 + t, HALO + columns - 1 - t, 2)
    halo_arrived(0)
    halo_arrived(1)
    for start in (0, HALO + columns):
        widen(start, HALO)
        for h in range(2):
            for level in range(2):
                by_columns(raw_u.at[level, h], wave_u.at[level, h], start, HALO)
    for t in range(steps):
        advance(t, 1 + t)
        advance(t, HALO + columns - 1 - t)

    def brighten(c, i):
        for h in range(2):
            a = [accel[t, h, pl.ds(c, BLOCK)] for t in range(steps)]
            store_rows(slab_i, h, i, sum(x * x for x in a))

    blocks(brighten, HALO, HALO + columns, 2)
    to_owners(slab_i, stage_i, back_i, 1)

    for copy in load_q:
        copy.wait()
    halo_arrived(2)
    for h in range(2):
        for level in range(2):
            by_columns(raw_q.at[level, h], wave_q.at[level, h], 0, ext)

    def retreat(k, c):
        n, laps = lap_both(wave_q, k + 1, c)
        for h in range(2):
            wave_q[k + 2, h, pl.ds(c + 1, BLOCK)] = (
                (n[h] + n[h]) - wave_q[k, h, pl.ds(c + 1, BLOCK)]
            ) + speed[h, pl.ds(c, BLOCK)] * laps[h]

    for k in range(steps):
        blocks(lambda c, i: retreat(k, c), HALO - 3 + k, HALO + columns + 3 - k, 3)

    def correlate(c, i):
        products = [
            sum(
                wave_q[steps + 1 - t, h, pl.ds(c + 1, BLOCK)] * accel[t, h, pl.ds(c, BLOCK)]
                for t in range(steps)
            )
            for h in range(2)
        ]
        store_rows(slab_d, 0, i, products[1])
        grad_part[pl.ds(i * BLOCK, BLOCK)] = products[0]

    blocks(correlate, HALO, HALO + columns, 2)
    to_owners(slab_d, stage_d, back_d, 2)

    for copy in load_r + load_b:
        copy.wait()
    halo_arrived(4)
    halo_arrived(5)
    halo_arrived(3)
    by_columns(raw_b.at[0], wave_b.at[0], 0, ext)
    by_columns(raw_b.at[1], wave_b.at[1], 0, ext)
    beside = HALO // 2
    heard = (
        [(0, n_rec - beside + r) for r in range(beside)]
        + [(1, r) for r in range(n_rec)]
        + [(2, r) for r in range(beside)]
    )
    for side in range(3):
        for t in range(steps):
            by_step[side, t] = obs[side, :, t, :]
    cells = [jnp.broadcast_to(rec[side], (shots, n_rec)) for side in range(3)]
    data = [[by_step[side, t] for t in range(steps)] for side in range(3)]
    for slot, (side, r) in enumerate(heard):
        cell = jnp.broadcast_to(cells[side][:, r : r + 1], (shots, LANES)) - first_cell - lane
        for t in range(steps):
            target[t, slot] = jnp.broadcast_to(data[side][t][:, r : r + 1], (shots, LANES))
        for w in range(2):
            c = 2 * slot + w
            mask[c] = jnp.where(cell == c * depth, 1.0, 0.0)

    box_arrived(tile_in, 0)
    for j in range(n_box + 6):
        owner = lax.rem(rotation + j - 3 + n_box, n_box)
        tile = tile_in[owner, j // n_box]
        for w in range(2):
            image[HALO - 6 + 2 * j + w] = jnp.broadcast_to(tile[w : w + 1], (shots, LANES))

    def scatter_wave(t, c):
        n, lap = lap_top(wave_b, t + 1, c, False)
        b = (
            ((n + n) - wave_b[t, pl.ds(c + 1, BLOCK)])
            + speed[0, pl.ds(c, BLOCK)] * lap
            + image[pl.ds(c, BLOCK)] * accel[t, 0, pl.ds(c, BLOCK)]
        )
        if t < steps - 1:
            wave_b[t + 2, pl.ds(c + 1, BLOCK)] = b
        recorded = target[t, pl.ds(c // 2, BLOCK // 2)]
        recorded = jnp.broadcast_to(
            recorded[:, None], (BLOCK // 2, 2, shots, LANES)
        ).reshape(BLOCK, shots, LANES)
        adj_m[t, pl.ds(c + 1, BLOCK)] = mask[pl.ds(c, BLOCK)] * (b - recorded)

    for t in range(steps):
        inset = 0 if t < 2 else HALO // 2
        count = (ext - 2 * inset) // BLOCK
        for i in range(count):
            scatter_wave(t, inset + i * BLOCK)

    from_boxes(back_i, aligned_i, 1)
    reduce_i[g] = aligned_i[mine]
    shot_exchange(lambda s: aligned_i.at[pl.ds(s * share, share)], reduce_i.at[g], 0)

    def misfit_wave(t):
        return adj_m.at[t] if t == steps - 1 else adj_r.at[t]

    def residual(t, c):
        n, sides = around(misfit_wave(t + 1), c)
        shallow = jnp.where(at_top, 0.0, turn(n, 1))
        deep = jnp.where(at_bottom, 0.0, turn(n, LANES - 1))
        lap = sides + (shallow + deep) - 4.0 * n
        q = (n + n) + speed[0, pl.ds(c, BLOCK)] * lap + adj_m[t, pl.ds(c + 1, BLOCK)]
        if t + 2 < steps:
            q = q - misfit_wave(t + 2)[pl.ds(c + 1, BLOCK)]
        adj_r[t, pl.ds(c + 1, BLOCK)] = q

    for t in reversed(range(steps - 1)):
        start, stop = HALO - t, HALO + columns + t
        count = -(-(stop - start) // BLOCK)
        for i in range(count):
            residual(t, min(start + i * BLOCK, stop - BLOCK))

    def correlate_late(c, i):
        total = grad_part[pl.ds(i * BLOCK, BLOCK)] + sum(
            misfit_wave(t)[pl.ds(c + 1, BLOCK)] * accel[t, 0, pl.ds(c, BLOCK)]
            for t in range(steps)
        )
        store_rows(slab_s, 0, i, total)

    for i in range(columns // BLOCK):
        correlate_late(HALO + i * BLOCK, i)
    to_owners(slab_s, stage_s, back_s, 3)

    from_boxes(back_d, aligned_d, 2)
    to_all(aligned_d, gather_d, 1)

    wait_bytes(reduce_i.at[pl.ds(0, n_shot - 1)], shot_recv.at[0])
    light = reduce_i[0]
    for s in range(1, n_shot):
        light = light + reduce_i[s]
    scale[mine] = jnp.sqrt(light + damping)
    shot_exchange(lambda s: scale.at[mine], scale.at[mine], 2)

    from_boxes(back_s, aligned_s, 3)
    to_all(aligned_s, gather_s, 3)

    def total_of(gathered, sem):
        wait_bytes(gathered.at[pl.ds(0, n_shot - 1)], shot_recv.at[sem])
        total = gathered[0, :, 0]
        for s in range(1, n_shot):
            total = total + gathered[s, :, 0]
        return total

    deep_total = total_of(gather_d, 1)
    wait_bytes(scale.at[others], shot_recv.at[2])
    out[:, 0, :, half[1]] = deep_total / scale[:, 1]
    out[:, 0, :, half[0]] = total_of(gather_s, 3) / scale[:, 0]

    for group in range(6):
        halo_sent(group)
    box_sent(tile_out, 0)
    box_sent(stage_i, 1)
    box_sent(stage_d, 2)
    box_sent(stage_s, 3)
    wait_bytes(aligned_i.at[others], shot_send.at[0])
    wait_bytes(gather_d.at[pl.ds(0, n_shot - 1)], shot_send.at[1])
    wait_bytes(scale.at[others], shot_send.at[2])
    wait_bytes(gather_s.at[pl.ds(0, n_shot - 1)], shot_send.at[3])


def on_device(
    n_box,
    n_shot,
    u_prev,
    u_now,
    born_prev,
    born_now,
    adj_after,
    adj_last,
    velocity,
    wavelet,
    sources,
    receivers,
    observed,
    first_tile,
    reflectivity,
):
    shots, columns, depth = u_now.shape[1:]
    steps = wavelet.shape[2]
    n_rec = receivers.shape[1]
    rounds = reflectivity.shape[0]
    ext = columns + 2 * HALO
    spare = rounds - n_box
    share = rounds // n_shot

    def vmem(*dims):
        return pltpu.VMEM(dims, F32)

    plane = (shots, LANES)
    tile = (2, LANES)
    scratch = [
        pltpu.SMEM(sources.shape, jnp.int32),
        pltpu.SMEM((1, steps, shots), F32),
        vmem(2, 2, shots, ext, LANES),
        vmem(2, 2, shots, ext, LANES),
        vmem(2, shots, ext, LANES),
        vmem(2, ext, LANES),
        pltpu.VMEM((3, 1, n_rec), jnp.int32),
        vmem(3, shots, steps, n_rec),
        vmem(rounds + 2, *tile),
        vmem(steps + 1, 2, ext + 2, *plane),
        vmem(steps, 2, ext, *plane),
        vmem(steps + 1, ext + 2, *plane),
        vmem(steps + 2, 2, ext + 2, *plane),
        vmem(columns, *plane),
        vmem(steps, ext + 2, *plane),
        vmem(2, ext, *plane),
        vmem(ext, *plane),
        vmem(ext, *plane),
        vmem(steps, ext // 2, *plane),
        vmem(3, steps, shots, n_rec),
        vmem(steps - 1, ext + 2, *plane),
        vmem(n_box, 2, *tile),
        vmem(n_box, 2, *tile),
        vmem(2 * n_box, 2, *tile),
        vmem(2 * n_box, 1, *tile),
        vmem(2 * n_box, 1, *tile),
        vmem(n_box, 2, *tile),
        vmem(n_box, 1, *tile),
        vmem(n_box, 1, *tile),
        vmem(n_box + 2 * spare, 2, *tile),
        vmem(n_box + 2 * spare, 1, *tile),
        vmem(n_box + 2 * spare, 1, *tile),
        vmem(rounds, 2, *tile),
        vmem(rounds, 1, *tile),
        vmem(rounds, 1, *tile),
        vmem(n_shot, share, 2, *tile),
        vmem(n_shot, rounds, 1, *tile),
        vmem(n_shot, rounds, 1, *tile),
        vmem(rounds, 2, *tile),
        pltpu.SemaphoreType.DMA((19,)),
        pltpu.SemaphoreType.DMA((2, 6)),
        pltpu.SemaphoreType.DMA((2, 6)),
        pltpu.SemaphoreType.DMA((4,)),
        pltpu.SemaphoreType.DMA((4,)),
        pltpu.SemaphoreType.DMA((4,)),
        pltpu.SemaphoreType.DMA((4,)),
    ]
    hbm = pl.BlockSpec(memory_space=pltpu.HBM)
    return pl.pallas_call(
        functools.partial(kernel, n_box, n_shot),
        out_shape=jax.ShapeDtypeStruct(reflectivity.shape, F32),
        in_specs=[pl.BlockSpec(memory_space=pltpu.SMEM)] + [hbm] * 12,
        out_specs=pl.BlockSpec(memory_space=pltpu.VMEM),
        scratch_shapes=scratch,
        compiler_params=pltpu.CompilerParams(
            collective_id=0, has_side_effects=True, vmem_limit_bytes=60 * 1024 * 1024
        ),
    )(
        first_tile,
        sources,
        jnp.transpose(wavelet, (0, 2, 1)),
        u_prev,
        u_now,
        born_prev,
        born_now,
        adj_after,
        adj_last,
        velocity,
        receivers,
        observed,
        reflectivity,
    )


def solution(mesh):
    return jax.shard_map(
        functools.partial(on_device, mesh.shape["box"], mesh.shape["shot"]),
        mesh=mesh,
        in_specs=(
            P("shot", None, "box", None),
            P("shot", None, "box", None),
            P("shot", None, "box", None),
            P("shot", None, "box", None),
            P("shot", None, "box", None),
            P("shot", None, "box", None),
            P("shot", "box", None),
            P("shot", None, None),
            P("shot", None),
            P("shot", "box"),
            P("shot", None, None, "box"),
            P("shot"),
            P(None, "box", None, None),
        ),
        out_specs=P(None, "box", None, None),
        check_vma=False,
    )
```

time: 46.4 us -> 41 us (0.88)
  Pallas kernels: 44 us -> 38.4 us
    pallas_call x1, Pallas kernels: 44 us -> 38.4 us  [on_device(): pl.pallas_call(functools.partial(kernel, n_box, n_shot), out_shape=jax.Sh...]
where the time goes in v3:
time: 41 us; the launch traced here: 40.6 us
  Pallas kernels  38.4 us (94%)
  local copies, waits for them, and re-layouts  1.53 us (4%)
  between operations  0.66 us (2%)
    pallas_call x1, Pallas kernels, on_device(): pl.pallas_call(functools.partial(kernel, n_box, n_shot), out_shape=jax.Sh...  38.4 us
    unnamed x1, local copies, waits for them, and re-layouts  1.53 us

profile of v3, /device:TPU:1, one launch (start us, length us, event | category | flops | bytes accessed | tf_op | source)
XLA Modules:
  0.0 40.6 jit_solution(10777175400594107159)
XLA Ops:
  0.7 38.4 %shard_map.127 = f32[40,1,2,256]{3,2,1,0:T(2,128)} custom-call(s32[1]{0:T(128)S(6)} %copy.15.first_tile, s32[1,8]{1,0:T(1,128)} %sources.1, f32[1,4,8]{2,1,0:T(4,128)} %bitcast.1, f32[1,8,64,256]{3,2,1,0:T(8,128)} %u_prev.1, f32[1,8,64,256]{3,2,1,0:T(8,128)} %u_now.1, f32[1,8,64,256]{3,2,1,0:T(8,128)} %born_prev.1, f32[1,8,64,256]{3,2,1,0:T(8,128)} %born_now.1, ...), custom_call_target="tpu_custom_call" | custom-call | tf_op jit(solution)/shard_map/pallas_call | solution.py:678
  39.0 1.5 %copy.16 = f32[40,1,2,256]{3,2,1,0:T(2,128)} copy(f32[40,1,2,256]{3,2,1,0:T(2,128)} %shard_map.127) | data formatting | bytes 163840

commit v4 on v3

--- a/solution.py
+++ b/solution.py
@@ -77,9 +77,9 @@
     aligned_d,
     aligned_s,
     reduce_i,
-    gather_d,
+    reduce_d,
     gather_s,
-    scale,
+    finished,
     load_sem,
     halo_send,
     halo_recv,
@@ -560,29 +560,29 @@
     to_owners(slab_s, stage_s, back_s, 3)
 
     from_boxes(back_d, aligned_d, 2)
-    to_all(aligned_d, gather_d, 1)
-
-    wait_bytes(reduce_i.at[pl.ds(0, n_shot - 1)], shot_recv.at[0])
-    light = reduce_i[0]
-    for s in range(1, n_shot):
-        light = light + reduce_i[s]
-    scale[mine] = jnp.sqrt(light + damping)
-    shot_exchange(lambda s: scale.at[mine], scale.at[mine], 2)
+    reduce_d[g] = aligned_d[mine]
+    shot_exchange(lambda s: aligned_d.at[pl.ds(s * share, share)], reduce_d.at[g], 1)
+
+    def total_of(gathered, sem):
+        wait_bytes(gathered.at[pl.ds(0, n_shot - 1)], shot_recv.at[sem])
+        total = gathered[0]
+        for s in range(1, n_shot):
+            total = total + gathered[s]
+        return total
+
+    light = jnp.sqrt(total_of(reduce_i, 0) + damping)
 
     from_boxes(back_s, aligned_s, 3)
     to_all(aligned_s, gather_s, 3)
 
-    def total_of(gathered, sem):
-        wait_bytes(gathered.at[pl.ds(0, n_shot - 1)], shot_recv.at[sem])
-        total = gathered[0, :, 0]
-        for s in range(1, n_shot):
-            total = total + gathered[s, :, 0]
-        return total
-
-    deep_total = total_of(gather_d, 1)
-    wait_bytes(scale.at[others], shot_recv.at[2])
-    out[:, 0, :, half[1]] = deep_total / scale[:, 1]
-    out[:, 0, :, half[0]] = total_of(gather_s, 3) / scale[:, 0]
+    finished[mine, 1] = total_of(reduce_d, 1)[:, 0] / light[:, 1]
+    finished[mine, 0] = light[:, 0]
+    shot_exchange(lambda s: finished.at[mine], finished.at[mine], 2)
+
+    shallow_total = total_of(gather_s, 3)[:, 0]
+    wait_bytes(finished.at[others], shot_recv.at[2])
+    out[:, 0, :, half[1]] = finished[:, 1]
+    out[:, 0, :, half[0]] = shallow_total / finished[:, 0]
 
     for group in range(6):
         halo_sent(group)
@@ -591,8 +591,8 @@
     box_sent(stage_d, 2)
     box_sent(stage_s, 3)
     wait_bytes(aligned_i.at[others], shot_send.at[0])
-    wait_bytes(gather_d.at[pl.ds(0, n_shot - 1)], shot_send.at[1])
-    wait_bytes(scale.at[others], shot_send.at[2])
+    wait_bytes(aligned_d.at[others], shot_send.at[1])
+    wait_bytes(finished.at[others], shot_send.at[2])
     wait_bytes(gather_s.at[pl.ds(0, n_shot - 1)], shot_send.at[3])
 
 
@@ -663,7 +663,7 @@
         vmem(rounds, 1, *tile),
         vmem(rounds, 1, *tile),
         vmem(n_shot, share, 2, *tile),
-        vmem(n_shot, rounds, 1, *tile),
+        vmem(n_shot, share, 1, *tile),
         vmem(n_shot, rounds, 1, *tile),
         vmem(rounds, 2, *tile),
         pltpu.SemaphoreType.DMA((19,)),

time: 41 us -> 41.5 us (1.012)
  Pallas kernels: 38.4 us -> 39.1 us
    pallas_call x1, Pallas kernels: 38.4 us -> 39.1 us  [on_device(): pl.pallas_call(functools.partial(kernel, n_box, n_shot), out_shape=jax.Sh...]
where the time goes in v4:
time: 41.5 us; the launch traced here: 41.3 us
  Pallas kernels  39.1 us (94%)
  local copies, waits for them, and re-layouts  1.53 us (4%)
  between operations  0.66 us (2%)
    pallas_call x1, Pallas kernels, on_device(): pl.pallas_call(functools.partial(kernel, n_box, n_shot), out_shape=jax.Sh...  39.1 us
    unnamed x1, local copies, waits for them, and re-layouts  1.53 us

profile of v4, /device:TPU:1, one launch (start us, length us, event | category | flops | bytes accessed | tf_op | source)
XLA Modules:
  0.0 41.3 jit_solution(4083915631678533401)
XLA Ops:
  0.7 39.1 %shard_map.127 = f32[40,1,2,256]{3,2,1,0:T(2,128)} custom-call(s32[1]{0:T(128)S(6)} %copy.15.first_tile, s32[1,8]{1,0:T(1,128)} %sources.1, f32[1,4,8]{2,1,0:T(4,128)} %bitcast.1, f32[1,8,64,256]{3,2,1,0:T(8,128)} %u_prev.1, f32[1,8,64,256]{3,2,1,0:T(8,128)} %u_now.1, f32[1,8,64,256]{3,2,1,0:T(8,128)} %born_prev.1, f32[1,8,64,256]{3,2,1,0:T(8,128)} %born_now.1, ...), custom_call_target="tpu_custom_call" | custom-call | tf_op jit(solution)/shard_map/pallas_call | solution.py:678
  39.8 1.5 %copy.16 = f32[40,1,2,256]{3,2,1,0:T(2,128)} copy(f32[40,1,2,256]{3,2,1,0:T(2,128)} %shard_map.127) | data formatting | bytes 163840

commit v5 on v3

--- a/solution.py
+++ b/solution.py
@@ -624,14 +624,15 @@
     def vmem(*dims):
         return pltpu.VMEM(dims, F32)
 
+    pitch = ext + HALO
     plane = (shots, LANES)
     tile = (2, LANES)
     scratch = [
         pltpu.SMEM(sources.shape, jnp.int32),
         pltpu.SMEM((1, steps, shots), F32),
-        vmem(2, 2, shots, ext, LANES),
-        vmem(2, 2, shots, ext, LANES),
-        vmem(2, shots, ext, LANES),
+        vmem(2, 2, shots, pitch, LANES),
+        vmem(2, 2, shots, pitch, LANES),
+        vmem(2, shots, pitch, LANES),
         vmem(2, ext, LANES),
         pltpu.VMEM((3, 1, n_rec), jnp.int32),
         vmem(3, shots, steps, n_rec),

time: 41 us -> 40.9 us (level)
  no operation moved by 1% of the time
where the time goes in v5:
time: 40.9 us; the launch traced here: 40.4 us
  Pallas kernels  38.2 us (93%)
  local copies, waits for them, and re-layouts  1.53 us (4%)
  between operations  0.66 us (2%)
    pallas_call x1, Pallas kernels, on_device(): pl.pallas_call(functools.partial(kernel, n_box, n_shot), out_shape=jax.Sh...  38.2 us
    unnamed x1, local copies, waits for them, and re-layouts  1.53 us

profile of v5, /device:TPU:1, one launch (start us, length us, event | category | flops | bytes accessed | tf_op | source)
XLA Modules:
  0.0 40.4 jit_solution(12543027519173765685)
XLA Ops:
  0.7 38.2 %shard_map.127 = f32[40,1,2,256]{3,2,1,0:T(2,128)} custom-call(s32[1]{0:T(128)S(6)} %copy.15.first_tile, s32[1,8]{1,0:T(1,128)} %sources.1, f32[1,4,8]{2,1,0:T(4,128)} %bitcast.1, f32[1,8,64,256]{3,2,1,0:T(8,128)} %u_prev.1, f32[1,8,64,256]{3,2,1,0:T(8,128)} %u_now.1, f32[1,8,64,256]{3,2,1,0:T(8,128)} %born_prev.1, f32[1,8,64,256]{3,2,1,0:T(8,128)} %born_now.1, ...), custom_call_target="tpu_custom_call" | custom-call | tf_op jit(solution)/shard_map/pallas_call | solution.py:679
  38.9 1.5 %copy.16 = f32[40,1,2,256]{3,2,1,0:T(2,128)} copy(f32[40,1,2,256]{3,2,1,0:T(2,128)} %shard_map.127) | data formatting | bytes 163840

commit v6 on v5

--- a/solution.py
+++ b/solution.py
@@ -74,12 +74,13 @@
     back_d,
     back_s,
     aligned_i,
-    aligned_d,
-    aligned_s,
     reduce_i,
     gather_d,
     gather_s,
     scale,
+    start_out,
+    start_in,
+    start_smem,
     load_sem,
     halo_send,
     halo_recv,
@@ -205,8 +206,11 @@
             for h in range(2)
         ]
         yield 1, [(velocity.at[0, edge, half[h]], raw_v.at[h, halo]) for h in range(2)]
+        shift = HALO // 2 if side == 0 else 0
+        near = pl.ds(edge.start + shift, HALO // 2)
+        there = pl.ds(halo.start + shift, HALO // 2)
         yield 2, [
-            (field.at[0, :, edge, half[h]], raw_q.at[f, h, :, halo])
+            (field.at[0, :, near, half[h]], raw_q.at[f, h, :, there])
             for f, field in enumerate((adj_after, adj_last))
             for h in range(2)
         ]
@@ -223,7 +227,7 @@
         return (
             raw_u.at[:, :, :, halo],
             raw_v.at[:, halo],
-            raw_q.at[:, :, :, halo],
+            raw_q.at[:, :, :, pl.ds(halo.start + (HALO // 2 if side == 0 else 0), HALO // 2)],
             raw_b.at[:, :, halo],
             rec.at[side],
             obs.at[side],
@@ -259,6 +263,8 @@
 
     send_halos((0, 1))
     box_exchange(tile_out, tile_in, p, 0)
+    start_out[...] = jnp.full((1, LANES), first_round, jnp.int32)
+    start_in[g] = start_out[...]
     send_halos((2, 3, 4, 5))
 
     blank = jnp.zeros((shots, LANES), F32)
@@ -269,7 +275,7 @@
             adj_m[level, pad] = blank
     for c in (0, 1, ext - 2, ext - 1):
         image[c] = blank
-    for back in (back_i, back_d, back_s):
+    for back in (back_i,):
         for place in (0, spare + n_box):
             back[pl.ds(place, spare)] = jnp.zeros((spare,) + back.shape[1:], F32)
 
@@ -368,10 +374,10 @@
 
     turned = lax.rem(n_box - rotation, n_box)
 
-    def to_owners(slab, staged, back, sem):
+    def to_owners(slab, staged, back, place, sem):
         staged[...] = slab[pl.ds(turned, n_box)]
-        back[spare + p] = staged[p]
-        box_exchange(staged, back, spare + p, sem)
+        back[place + p] = staged[p]
+        box_exchange(staged, back, place + p, sem)
 
     def from_boxes(back, aligned, sem):
         box_arrived(back, sem)
@@ -392,10 +398,13 @@
 
         lax.fori_loop(1, n_shot, send, 0)
 
-    def to_all(aligned, gathered, sem):
-        shot_exchange(lambda s: aligned, gathered.at[g], sem)
-        gathered[g] = aligned[...]
-
+    filled = pl.ds(spare, n_box)
+
+    def to_all(back, gathered, sem):
+        shot_exchange(lambda s: back, gathered.at[g, filled], sem)
+        gathered[g, filled] = back[...]
+
+    shot_exchange(lambda s: start_out, start_in.at[g], 4)
     mine = pl.ds(g * share, share)
     others = pl.ds(0, (n_shot - 1) * share)
     cell_step = lax.broadcasted_iota(jnp.int32, (BLOCK, shots, LANES), 0) * depth
@@ -438,7 +447,7 @@
             store_rows(slab_i, h, i, sum(x * x for x in a))
 
     blocks(brighten, HALO, HALO + columns, 2)
-    to_owners(slab_i, stage_i, back_i, 1)
+    to_owners(slab_i, stage_i, back_i, spare, 1)
 
     for copy in load_q:
         copy.wait()
@@ -469,7 +478,7 @@
         grad_part[pl.ds(i * BLOCK, BLOCK)] = products[0]
 
     blocks(correlate, HALO, HALO + columns, 2)
-    to_owners(slab_d, stage_d, back_d, 2)
+    to_owners(slab_d, stage_d, back_d, 0, 2)
 
     for copy in load_r + load_b:
         copy.wait()
@@ -557,10 +566,18 @@
 
     for i in range(columns // BLOCK):
         correlate_late(HALO + i * BLOCK, i)
-    to_owners(slab_s, stage_s, back_s, 3)
-
-    from_boxes(back_d, aligned_d, 2)
-    to_all(aligned_d, gather_d, 1)
+    to_owners(slab_s, stage_s, back_s, 0, 3)
+
+    box_arrived(back_d, 2)
+    to_all(back_d, gather_d, 1)
+    wait_bytes(start_in.at[pl.ds(0, n_shot - 1)], shot_recv.at[4])
+    load_starts = pltpu.make_async_copy(start_in, start_smem, load_sem.at[19])
+    load_starts.start()
+    for gathered in (gather_d, gather_s):
+        for place in (0, spare + n_box):
+            for s in range(n_shot):
+                gathered[s, pl.ds(place, spare)] = jnp.zeros((spare, 1, 2, LANES), F32)
+    load_starts.wait()
 
     wait_bytes(reduce_i.at[pl.ds(0, n_shot - 1)], shot_recv.at[0])
     light = reduce_i[0]
@@ -569,15 +586,14 @@
     scale[mine] = jnp.sqrt(light + damping)
     shot_exchange(lambda s: scale.at[mine], scale.at[mine], 2)
 
-    from_boxes(back_s, aligned_s, 3)
-    to_all(aligned_s, gather_s, 3)
+    box_arrived(back_s, 3)
+    to_all(back_s, gather_s, 3)
 
     def total_of(gathered, sem):
-        wait_bytes(gathered.at[pl.ds(0, n_shot - 1)], shot_recv.at[sem])
-        total = gathered[0, :, 0]
-        for s in range(1, n_shot):
-            total = total + gathered[s, :, 0]
-        return total
+        wait_bytes(gathered.at[pl.ds(0, n_shot - 1), filled], shot_recv.at[sem])
+        return sum(
+            gathered[s, pl.ds(spare - start_smem[s, 0, 0], rounds), 0] for s in range(n_shot)
+        )
 
     deep_total = total_of(gather_d, 1)
     wait_bytes(scale.at[others], shot_recv.at[2])
@@ -591,9 +607,10 @@
     box_sent(stage_d, 2)
     box_sent(stage_s, 3)
     wait_bytes(aligned_i.at[others], shot_send.at[0])
-    wait_bytes(gather_d.at[pl.ds(0, n_shot - 1)], shot_send.at[1])
+    wait_bytes(gather_d.at[pl.ds(0, n_shot - 1), filled], shot_send.at[1])
     wait_bytes(scale.at[others], shot_send.at[2])
-    wait_bytes(gather_s.at[pl.ds(0, n_shot - 1)], shot_send.at[3])
+    wait_bytes(gather_s.at[pl.ds(0, n_shot - 1), filled], shot_send.at[3])
+    wait_bytes(start_in.at[pl.ds(0, n_shot - 1)], shot_send.at[4])
 
 
 def on_device(
@@ -658,22 +675,23 @@
         vmem(n_box, 1, *tile),
         vmem(n_box, 1, *tile),
         vmem(n_box + 2 * spare, 2, *tile),
-        vmem(n_box + 2 * spare, 1, *tile),
-        vmem(n_box + 2 * spare, 1, *tile),
+        vmem(n_box, 1, *tile),
+        vmem(n_box, 1, *tile),
         vmem(rounds, 2, *tile),
-        vmem(rounds, 1, *tile),
-        vmem(rounds, 1, *tile),
         vmem(n_shot, share, 2, *tile),
-        vmem(n_shot, rounds, 1, *tile),
-        vmem(n_shot, rounds, 1, *tile),
+        vmem(n_shot, n_box + 2 * spare, 1, *tile),
+        vmem(n_shot, n_box + 2 * spare, 1, *tile),
         vmem(rounds, 2, *tile),
-        pltpu.SemaphoreType.DMA((19,)),
+        pltpu.VMEM((1, LANES), jnp.int32),
+        pltpu.VMEM((n_shot, 1, LANES), jnp.int32),
+        pltpu.SMEM((n_shot, 1, LANES), jnp.int32),
+        pltpu.SemaphoreType.DMA((20,)),
         pltpu.SemaphoreType.DMA((2, 6)),
         pltpu.SemaphoreType.DMA((2, 6)),
         pltpu.SemaphoreType.DMA((4,)),
         pltpu.SemaphoreType.DMA((4,)),
-        pltpu.SemaphoreType.DMA((4,)),
-        pltpu.SemaphoreType.DMA((4,)),
+        pltpu.SemaphoreType.DMA((5,)),
+        pltpu.SemaphoreType.DMA((5,)),
     ]
     hbm = pl.BlockSpec(memory_space=pltpu.HBM)
     return pl.pallas_call(

time: 40.9 us -> 39.1 us (0.956)
  Pallas kernels: 38.2 us -> 36.7 us
    pallas_call x1, Pallas kernels: 38.2 us -> 36.7 us  [on_device(): pl.pallas_call(functools.partial(kernel, n_box, n_shot), out_shape=jax.Sh...]
where the time goes in v6:
time: 39.1 us; the launch traced here: 38.9 us
  Pallas kernels  36.7 us (94%)
  local copies, waits for them, and re-layouts  1.53 us (4%)
  between operations  0.66 us (2%)
    pallas_call x1, Pallas kernels, on_device(): pl.pallas_call(functools.partial(kernel, n_box, n_shot), out_shape=jax.Sh...  36.7 us
    unnamed x1, local copies, waits for them, and re-layouts  1.53 us

profile of v6, /device:TPU:1, one launch (start us, length us, event | category | flops | bytes accessed | tf_op | source)
XLA Modules:
  0.0 38.9 jit_solution(16026836925392005679)
XLA Ops:
  0.7 36.7 %shard_map.127 = f32[40,1,2,256]{3,2,1,0:T(2,128)} custom-call(s32[1]{0:T(128)S(6)} %copy.15.first_tile, s32[1,8]{1,0:T(1,128)} %sources.1, f32[1,4,8]{2,1,0:T(4,128)} %bitcast.1, f32[1,8,64,256]{3,2,1,0:T(8,128)} %u_prev.1, f32[1,8,64,256]{3,2,1,0:T(8,128)} %u_now.1, f32[1,8,64,256]{3,2,1,0:T(8,128)} %born_prev.1, f32[1,8,64,256]{3,2,1,0:T(8,128)} %born_now.1, ...), custom_call_target="tpu_custom_call" | custom-call | tf_op jit(solution)/shard_map/pallas_call | solution.py:697
  37.4 1.5 %copy.16 = f32[40,1,2,256]{3,2,1,0:T(2,128)} copy(f32[40,1,2,256]{3,2,1,0:T(2,128)} %shard_map.127) | data formatting | bytes 163840

commit v7 on v6

--- a/solution.py
+++ b/solution.py
@@ -114,8 +114,8 @@
         )
         return carry
 
-    lax.fori_loop(1, n_box, greet_box, 0)
-    lax.fori_loop(1, n_shot, greet_shot, 0)
+    lax.fori_loop(1, n_box, greet_box, 0, unroll=n_box - 1)
+    lax.fori_loop(1, n_shot, greet_shot, 0, unroll=n_shot - 1)
 
     loads = []
 
@@ -188,7 +188,7 @@
             ).start()
             return carry
 
-        lax.fori_loop(1, n_box, send, 0)
+        lax.fori_loop(1, n_box, send, 0, unroll=n_box - 1)
 
     def box_sent(staged, sem):
         wait_bytes(staged.at[pl.ds(0, n_box - 1)], box_send.at[sem])
@@ -396,7 +396,7 @@
             ).start()
             return carry
 
-        lax.fori_loop(1, n_shot, send, 0)
+        lax.fori_loop(1, n_shot, send, 0, unroll=n_shot - 1)
 
     filled = pl.ds(spare, n_box)
 
@@ -429,7 +429,7 @@
         for level in range(2):
             by_columns(raw_u.at[level, h], wave_u.at[level, h], HALO, columns)
     for t in range(steps):
-        blocks(lambda c, i: advance(t, c), HALO + 1 + t, HALO + columns - 1 - t, 2)
+        blocks(lambda c, i: advance(t, c), HALO + 1 + t, HALO + columns - 1 - t, 8 if t < 3 else 7)
     halo_arrived(0)
     halo_arrived(1)
     for start in (0, HALO + columns):
@@ -464,7 +464,7 @@
             ) + speed[h, pl.ds(c, BLOCK)] * laps[h]
 
     for k in range(steps):
-        blocks(lambda c, i: retreat(k, c), HALO - 3 + k, HALO + columns + 3 - k, 3)
+        blocks(lambda c, i: retreat(k, c), HALO - 3 + k, HALO + columns + 3 - k, 9 if k < 3 else 8)
 
     def correlate(c, i):
         products = [

time: 39.1 us -> 36.4 us (0.931)
  Pallas kernels: 36.7 us -> 34 us
    pallas_call x1, Pallas kernels: 36.7 us -> 34 us  [on_device(): pl.pallas_call(functools.partial(kernel, n_box, n_shot), out_shape=jax.Sh...]
where the time goes in v7:
time: 36.4 us; the launch traced here: 36.2 us
  Pallas kernels  34 us (93%)
  local copies, waits for them, and re-layouts  1.53 us (4%)
  between operations  0.66 us (2%)
    pallas_call x1, Pallas kernels, on_device(): pl.pallas_call(functools.partial(kernel, n_box, n_shot), out_shape=jax.Sh...  34 us
    unnamed x1, local copies, waits for them, and re-layouts  1.53 us

profile of v7, /device:TPU:1, one launch (start us, length us, event | category | flops | bytes accessed | tf_op | source)
XLA Modules:
  0.0 36.2 jit_solution(5539867102078901000)
XLA Ops:
  0.7 34.0 %shard_map.127 = f32[40,1,2,256]{3,2,1,0:T(2,128)} custom-call(s32[1]{0:T(128)S(6)} %copy.15.first_tile, s32[1,8]{1,0:T(1,128)} %sources.1, f32[1,4,8]{2,1,0:T(4,128)} %bitcast.1, f32[1,8,64,256]{3,2,1,0:T(8,128)} %u_prev.1, f32[1,8,64,256]{3,2,1,0:T(8,128)} %u_now.1, f32[1,8,64,256]{3,2,1,0:T(8,128)} %born_prev.1, f32[1,8,64,256]{3,2,1,0:T(8,128)} %born_now.1, ...), custom_call_target="tpu_custom_call" | custom-call | tf_op jit(solution)/shard_map/pallas_call | solution.py:697
  34.7 1.5 %copy.16 = f32[40,1,2,256]{3,2,1,0:T(2,128)} copy(f32[40,1,2,256]{3,2,1,0:T(2,128)} %shard_map.127) | data formatting | bytes 163840

commit v8 on v7

--- a/solution.py
+++ b/solution.py
@@ -308,7 +308,7 @@
             working[start + c + 1] = column_of(raw, start + c)
             return carry
 
-        lax.fori_loop(0, count, move, 0, unroll=min(count, 16))
+        lax.fori_loop(0, count, move, 0, unroll=count)
 
     def widen(start, count):
         for h in range(2):
@@ -319,7 +319,7 @@
                 )
                 return carry
 
-            lax.fori_loop(0, count, spread, 0, unroll=min(count, 16))
+            lax.fori_loop(0, count, spread, 0, unroll=count)
 
     for copy in load_s:
         copy.wait()
@@ -446,7 +446,7 @@
             a = [accel[t, h, pl.ds(c, BLOCK)] for t in range(steps)]
             store_rows(slab_i, h, i, sum(x * x for x in a))
 
-    blocks(brighten, HALO, HALO + columns, 2)
+    blocks(brighten, HALO, HALO + columns, 8)
     to_owners(slab_i, stage_i, back_i, spare, 1)
 
     for copy in load_q:
@@ -477,7 +477,7 @@
         store_rows(slab_d, 0, i, products[1])
         grad_part[pl.ds(i * BLOCK, BLOCK)] = products[0]
 
-    blocks(correlate, HALO, HALO + columns, 2)
+    blocks(correlate, HALO, HALO + columns, 8)
     to_owners(slab_d, stage_d, back_d, 0, 2)
 
     for copy in load_r + load_b:

time: 36.4 us -> 36.2 us (level)
  no operation moved by 1% of the time
where the time goes in v8:
time: 36.2 us; the launch traced here: 36.1 us
  Pallas kernels  33.9 us (94%)
  local copies, waits for them, and re-layouts  1.53 us (4%)
  between operations  0.66 us (2%)
    pallas_call x1, Pallas kernels, on_device(): pl.pallas_call(functools.partial(kernel, n_box, n_shot), out_shape=jax.Sh...  33.9 us
    unnamed x1, local copies, waits for them, and re-layouts  1.53 us

profile of v8, /device:TPU:1, one launch (start us, length us, event | category | flops | bytes accessed | tf_op | source)
XLA Modules:
  0.0 36.1 jit_solution(16935782508110240979)
XLA Ops:
  0.7 33.9 %shard_map.127 = f32[40,1,2,256]{3,2,1,0:T(2,128)} custom-call(s32[1]{0:T(128)S(6)} %copy.15.first_tile, s32[1,8]{1,0:T(1,128)} %sources.1, f32[1,4,8]{2,1,0:T(4,128)} %bitcast.1, f32[1,8,64,256]{3,2,1,0:T(8,128)} %u_prev.1, f32[1,8,64,256]{3,2,1,0:T(8,128)} %u_now.1, f32[1,8,64,256]{3,2,1,0:T(8,128)} %born_prev.1, f32[1,8,64,256]{3,2,1,0:T(8,128)} %born_now.1, ...), custom_call_target="tpu_custom_call" | custom-call | tf_op jit(solution)/shard_map/pallas_call | solution.py:697
  34.6 1.5 %copy.16 = f32[40,1,2,256]{3,2,1,0:T(2,128)} copy(f32[40,1,2,256]{3,2,1,0:T(2,128)} %shard_map.127) | data formatting | bytes 163840
